TPU v7x, 512 devices: a whole 4x8x8 slice. The times are simulated.
512 devices in a mesh: rep: 16 (over y_hi, x, core), shard: 32 (over y_lo, z).
Axes of the slice: x: 4, y: 8 (y_hi: 2, y_lo: 4; y = y_hi * 4 + y_lo), z: 8, core: 2. Of those that a mesh axis runs over, the one named last changes fastest.
Arguments:
- grad_blocks: float32 [16, 1664, 2048], P('rep', None, 'shard'), may hold values from -2400 to 2400
- gain_grads: float32 [16, 12800], P('rep', 'shard'), may hold values from -240 to 240
- first_moment: float32 [32, 106896], P('shard'), may hold values from -6 to 6
- second_moment: float32 [32, 106896], P('shard'), may hold values from 0.25 to 4
- master_flat: float32 [32, 106896], P('shard'), may hold values from -6 to 6
- ema_flat: float32 [32, 106896], P('shard'), may hold values from -6 to 6
Outputs:
- new_first: float32 [32, 106896], P('shard')
- new_second: float32 [32, 106896], P('shard')
- new_master: float32 [32, 106896], P('shard')
- new_ema: float32 [32, 106896], P('shard')
- weight_blocks: bfloat16 [2, 1664, 2048], P(None, None, 'shard')
- gains: bfloat16 [12800], replicated
All inputs are finite; a program needn't handle non-finite values.
Results may differ from a plain program's by a relative error of at most 0.0004.
Values may be sent and summed in bfloat16 or wider, within the bound.
A program may use at most 64 MiB of HBM per device.

v0:
```python
import jax
import jax.numpy as jnp
from jax import lax
from jax.sharding import PartitionSpec as P

STEP = 100
PARAMS = 3420672


beta_one = 0.9
beta_two = 0.95
adam_eps = 1e-08
learn_rate = 0.02
weight_decay = 0.1
ema_keep = 0.95
clip_eps = 1e-06


def shards(grad_blocks, gain_grads, first_moment, second_moment, master_flat, ema_flat):
    replicas = lax.axis_size("rep")
    matrix_part = grad_blocks[0]
    small_part = gain_grads[0]
    matrix_part, small_part = lax.psum((matrix_part, small_part), "rep")
    owned = lax.all_to_all(matrix_part, "shard", split_axis=0, concat_axis=1, tiled=True)
    partial_value = jnp.sum(owned * owned) + jnp.sum(small_part * small_part)
    total = lax.psum(partial_value, "shard") / (replicas * replicas)
    main_len = owned.shape[0] * owned.shape[1]
    grads = jnp.concatenate([owned.reshape(main_len), small_part]).reshape(1, -1) / replicas
    rms = jnp.sqrt(total / PARAMS)
    clip = jnp.minimum(1.0, 1.0 / (rms + clip_eps))
    clipped = grads * clip
    new_first = beta_one * first_moment + (1.0 - beta_one) * clipped
    new_second = beta_two * second_moment + (1.0 - beta_two) * clipped * clipped
    update = (
        new_first
        / (1.0 - beta_one**STEP)
        / (jnp.sqrt(new_second / (1.0 - beta_two**STEP)) + adam_eps)
    )
    column = jnp.arange(grads.shape[1], dtype=jnp.int32)[None, :]
    decayed = jnp.where(column < main_len, weight_decay * master_flat, 0.0)
    new_master = master_flat - learn_rate * (update + decayed)
    new_ema = ema_keep * ema_flat + (1.0 - ema_keep) * new_master
    weights = new_master[0, :main_len].reshape(owned.shape).astype(jnp.bfloat16)
    averaged = new_ema[0, :main_len].reshape(owned.shape).astype(jnp.bfloat16)
    stacked = jnp.stack([weights, averaged], axis=0)
    weight_blocks = lax.all_to_all(stacked, "shard", split_axis=2, concat_axis=1, tiled=True)
    gains = lax.all_gather(
        new_master[0, main_len:].astype(jnp.bfloat16), "shard", axis=0, tiled=True
    )
    return (new_first, new_second, new_master, new_ema, weight_blocks, gains)


def solution(mesh):
    return jax.shard_map(
        shards,
        mesh=mesh,
        in_specs=(
            P("rep", None, "shard"),
            P("rep", "shard"),
            P("shard", None),
            P("shard", None),
            P("shard", None),
            P("shard", None),
        ),
        out_specs=(
            P("shard", None),
            P("shard", None),
            P("shard", None),
            P("shard", None),
            P(None, None, "shard"),
            P(),
        ),
        check_vma=False,
    )
```

profile of v0, /device:TPU:6, one launch (start us, length us, event | category | flops | bytes accessed | tf_op | source)
XLA Modules:
  0.0 529.7 jit_solution(15047340786175874549)
XLA Ops:
  7.2 0.0 all-reduce.3.cloned.1.call-start
  7.2 3.5 all_to_all.25
  10.8 0.0 all-reduce.3.cloned.1.call-update
  10.8 186.8 %all-reduce.3.cloned.1.call-done = f32[32,52,64]{1,0,2:T(8,128)} async-done(((f32[32,52,64]{1,0,2:T(8,128)}), f32[32,52,64]{1,0,2:T(8,128)}) %all-reduce.3.cloned.1.call-update) | async-done | bytes 426000 | tf_op jit(solution)/shard_map/psum | solution.py:23
  197.6 1.8 copy.33
  199.4 0.0 copy-start.7
  199.4 1.3 reshape.115
  200.7 7.9 %all-to-all-start = ((f32[32,1,3328]{2,1,0:T(1,128)}), f32[32,1,3328]{2,1,0:T(1,128)S(1)}, u32[]{:S(2)}, u32[]{:S(2)}) async-start(f32[32,1,3328]{2,1,0:T(1,128)} %reshape.115), calls=%async_computation | async-start | bytes 851968 | tf_op jit(solution)/shard_map/all_to_all | solution.py:24
  208.6 0.0 copy-done.7
  208.6 41.7 %psum.22 = f32[400]{0:T(512)S(1)} all-reduce(f32[400]{0:T(512)S(1)} %bitcast.23), channel_id=1, replica_groups=mesh['rep'=16,'shard'=32] {'rep'}, use_global_device_ids=true, to_apply=%region_1.0 | all-reduce | flops 400 | bytes 3200 | tf_op jit(solution)/shard_map/psum | solution.py:23
  250.3 0.6 multiply_reduce_fusion.1
  250.9 0.0 all-to-all-done
  250.9 0.5 broadcast.66
  251.4 1.6 reduce.7
  253.1 0.3 reshape.116
  253.4 0.8 multiply_reduce_fusion
  255.5 80.8 %psum.23 = f32[]{:T(128)} all-reduce(f32[]{:T(128)S(6)} %add.30), channel_id=1, replica_groups=mesh['rep'=16,'shard'=32] {'shard'}, use_global_device_ids=true, to_apply=%region_4.0 | all-reduce | flops 1 | bytes 8 | tf_op jit(solution)/shard_map/psum | solution.py:26
  337.0 0.0 copy-start.6
  337.0 0.2 copy.34
  337.2 0.0 copy-start.4
  337.2 0.0 copy-start.5
  337.2 0.5 concatenate.18
  337.8 0.3 copy-done.6
  338.0 0.2 copy-done.4
  338.3 0.1 copy-done.5
  338.4 5.0 fusion.3
  343.4 0.0 copy-start.1
  343.4 0.0 copy-start
  343.4 0.0 copy-start.3
  343.4 0.7 copy-done.1
  344.1 1.2 slice_reduce_fusion
  345.3 0.1 convert_element_type.26
  345.5 0.0 copy-done.3
  345.5 0.7 multiply_add_fusion
  346.2 0.0 copy-done
  346.2 0.0 copy-start.2
  346.2 0.7 copy-done.2
  347.0 1.1 fusion.2
  348.1 0.1 convert_element_type.27
  348.2 0.8 copy.36
  349.1 0.8 copy.35
  349.9 2.8 fusion.5
  352.7 3.5 reshape.117
  356.3 3.9 all-to-all-start.1
  360.2 1.3 dynamic-slice
  362.1 0.7 slice_reduce_fusion.1
  362.8 0.3 dynamic-update-slice
  363.1 153.1 %all-reduce = bf16[12800]{0:T(1024)(128)(2,1)} all-reduce(bf16[12800]{0:T(1024)(128)(2,1)S(1)} %dynamic-update-slice), channel_id=2, replica_groups=mesh['rep'=16,'shard'=32] {'shard'}, use_global_device_ids=true, to_apply=%add | all-reduce | flops 12800 | bytes 51200 | tf_op jit(solution)/shard_map/all_gather | solution.py:47
  516.2 0.0 all-to-all-done.1
  516.2 3.3 reshape.118
  519.5 0.7 copy.42
  520.2 2.7 all_to_all.31
  (1 shorter events, 0.0 us)
Async XLA Ops:
  7.2 190.4 %all-reduce.3.cloned.1.call-start = ((), (), s32[]{:S(2)}) async-start(), calls=%async_computation.2 | async-start | bytes 2097152 | tf_op jit(solution)/shard_map/psum | solution.py:23
  199.4 9.2 %copy-start.7 = (f32[1,400]{1,0:T(1,128)S(1)}, f32[1,400]{1,0:T(1,128)}, u32[]{:S(2)}) copy-start(f32[1,400]{1,0:T(1,128)} %param.7) | copy-start | bytes 4804
  200.7 50.2 %all-to-all-start = ((f32[32,1,3328]{2,1,0:T(1,128)}), f32[32,1,3328]{2,1,0:T(1,128)S(1)}, u32[]{:S(2)}, u32[]{:S(2)}) async-start(f32[32,1,3328]{2,1,0:T(1,128)} %reshape.115), calls=%async_computation | async-start | bytes 851968 | tf_op jit(solution)/shard_map/all_to_all | solution.py:24
  337.0 1.0 copy-start.6
  337.2 1.0 copy-start.4
  337.2 1.2 copy-start.5
  343.4 0.8 copy-start.1
  343.4 2.9 copy-start
  343.4 2.1 copy-start.3
  346.2 0.8 copy-start.2
  356.3 159.9 %all-to-all-start.1 = ((bf16[32,2,3328]{2,1,0:T(2,128)(2,1)}), bf16[32,2,3328]{2,1,0:T(2,128)(2,1)S(1)}, u32[]{:S(2)}, u32[]{:S(2)}) async-start(bf16[32,2,3328]{2,1,0:T(2,128)(2,1)} %reshape.117), calls=%async_computation.1 | async-start | bytes 851968 | tf_op jit(solution)/shard_map/all_to_all | solution.py:46
Sparse Core Ops, SparseCore 0:
  10.9 186.6 all-reduce.2
where the time goes:
time: 538 us; the launch traced here: 530 us
  blocking collectives  276 us (51%)
  waiting for transfers between devices  187 us (35%)
  local copies, waits for them, and re-layouts  26.9 us (5%)
  between operations  16.9 us (3%)
  starting transfers between devices  11.8 us (2%)
  other arithmetic  11.6 us (2%)
    psum x1, waiting for transfers between devices, shards(): matrix_part, small_part = lax.psum((matrix_part, small_part), 'rep')  187 us
    all_gather x1, blocking collectives, shards(): lax.all_gather(new_master[0, main_len:].astype(jnp.bfloat16), 'shard', ax...  153 us
    psum x1, blocking collectives, shards(): total = lax.psum(partial_value, 'shard') / (replicas * replicas)  80.8 us
    psum x1, blocking collectives, shards(): matrix_part, small_part = lax.psum((matrix_part, small_part), 'rep')  41.7 us
    unnamed x23, local copies, waits for them, and re-layouts  12.1 us
  transfers between devices with their start and end apart: 3, of which 1 were waited for; matrix products, arithmetic and copies ran while one was open for 1% of the time, Pallas kernels for 0%

commit v1 on v0

--- a/solution.py
+++ b/solution.py
@@ -15,16 +15,52 @@
 ema_keep = 0.95
 clip_eps = 1e-06
 
+LANE = 128
+
+
+def _pad_to(n):
+    return -(-n // LANE) * LANE
+
+
+def rep_sum(flat, replicas):
+    n = flat.shape[0]
+    chunk = n // replicas
+    width = _pad_to(chunk)
+    pieces = jnp.pad(flat.reshape(replicas, chunk), ((0, 0), (0, width - chunk)))
+    got = lax.all_to_all(pieces, "rep", split_axis=0, concat_axis=0, tiled=True)
+    mine = jnp.sum(got, axis=0)
+    every = jnp.broadcast_to(mine[None], (replicas, width))
+    full = lax.all_to_all(every, "rep", split_axis=0, concat_axis=0, tiled=True)
+    return full[:, :chunk].reshape(n)
+
 
 def shards(grad_blocks, gain_grads, first_moment, second_moment, master_flat, ema_flat):
     replicas = lax.axis_size("rep")
-    matrix_part = grad_blocks[0]
-    small_part = gain_grads[0]
-    matrix_part, small_part = lax.psum((matrix_part, small_part), "rep")
-    owned = lax.all_to_all(matrix_part, "shard", split_axis=0, concat_axis=1, tiled=True)
-    partial_value = jnp.sum(owned * owned) + jnp.sum(small_part * small_part)
-    total = lax.psum(partial_value, "shard") / (replicas * replicas)
-    main_len = owned.shape[0] * owned.shape[1]
+    owners = lax.axis_size("shard")
+    rows, cols = grad_blocks.shape[1], grad_blocks.shape[2]
+    small = gain_grads.shape[1]
+    main_block = rows * cols
+    flat = jnp.concatenate([grad_blocks[0].reshape(main_block), gain_grads[0]])
+    summed = rep_sum(flat, replicas)
+    matrix_part = summed[:main_block].reshape(rows, cols)
+    small_part = summed[main_block:]
+    partial_value = jnp.sum(matrix_part * matrix_part) + jnp.sum(small_part * small_part)
+
+    own_rows = rows // owners
+    piece = own_rows * cols
+    width = _pad_to(piece + 1)
+    send = jnp.concatenate(
+        [
+            matrix_part.reshape(owners, piece),
+            jnp.broadcast_to(partial_value, (owners, 1)),
+            jnp.zeros((owners, width - piece - 1), jnp.float32),
+        ],
+        axis=1,
+    )
+    got = lax.all_to_all(send, "shard", split_axis=0, concat_axis=0, tiled=True)
+    total = jnp.sum(got[:, piece]) / (replicas * replicas)
+    owned = got[:, :piece].reshape(owners, own_rows, cols).transpose(1, 0, 2)
+    main_len = own_rows * owners * cols
     grads = jnp.concatenate([owned.reshape(main_len), small_part]).reshape(1, -1) / replicas
     rms = jnp.sqrt(total / PARAMS)
     clip = jnp.minimum(1.0, 1.0 / (rms + clip_eps))
@@ -40,13 +76,25 @@
     decayed = jnp.where(column < main_len, weight_decay * master_flat, 0.0)
     new_master = master_flat - learn_rate * (update + decayed)
     new_ema = ema_keep * ema_flat + (1.0 - ema_keep) * new_master
-    weights = new_master[0, :main_len].reshape(owned.shape).astype(jnp.bfloat16)
-    averaged = new_ema[0, :main_len].reshape(owned.shape).astype(jnp.bfloat16)
-    stacked = jnp.stack([weights, averaged], axis=0)
-    weight_blocks = lax.all_to_all(stacked, "shard", split_axis=2, concat_axis=1, tiled=True)
-    gains = lax.all_gather(
-        new_master[0, main_len:].astype(jnp.bfloat16), "shard", axis=0, tiled=True
+    weights = new_master[0, :main_len].astype(jnp.bfloat16)
+    averaged = new_ema[0, :main_len].astype(jnp.bfloat16)
+    stacked = jnp.stack([weights, averaged], axis=0).reshape(2, own_rows, owners, cols)
+    back = stacked.transpose(2, 0, 1, 3).reshape(owners, 2 * piece)
+    gains_mine = new_master[0, main_len:].astype(jnp.bfloat16)
+    width2 = _pad_to(2 * piece + small)
+    send2 = jnp.concatenate(
+        [
+            back,
+            jnp.broadcast_to(gains_mine[None], (owners, small)),
+            jnp.zeros((owners, width2 - 2 * piece - small), jnp.bfloat16),
+        ],
+        axis=1,
     )
+    got2 = lax.all_to_all(send2, "shard", split_axis=0, concat_axis=0, tiled=True)
+    weight_blocks = (
+        got2[:, : 2 * piece].reshape(owners, 2, own_rows, cols).transpose(1, 0, 2, 3).reshape(2, rows, cols)
+    )
+    gains = got2[:, 2 * piece : 2 * piece + small].reshape(owners * small)
     return (new_first, new_second, new_master, new_ema, weight_blocks, gains)
 
 

time: 538 us -> 124 us (0.23); the launches traced: 530 us -> 123 us
  waiting for transfers between devices: 187 us -> 0 us
  blocking collectives: 276 us -> 93.6 us
  between operations: 16.9 us -> 2.97 us
  starting transfers between devices: 11.8 us -> 0 us
  local copies, waits for them, and re-layouts: 26.9 us -> 17.2 us
    psum x1 -> x0, waiting for transfers between devices: 187 us -> none  [shards(): matrix_part, small_part = lax.psum((matrix_part, small_part), 'rep')]
    all_gather x1 -> x0, blocking collectives: 153 us -> none  [shards(): lax.all_gather(new_master[0, main_len:].astype(jnp.bfloat16), 'shard', ax...]
    psum x2 -> x0, blocking collectives: 122 us -> none  [the longest x1 80.8 us: shards(): total = lax.psum(partial_value, 'shard') / (replicas * replicas)]
    all_to_all x0 -> x4, blocking collectives: none -> 93.6 us  [the longest x1 32.8 us: shards(): got = lax.all_to_all(send, 'shard', split_axis=0, concat_axis=0, tiled=True)]
    all_to_all x2 -> x0, starting transfers between devices: 11.8 us -> none  [the longest x1 7.9 us: shards(): lax.all_to_all(matrix_part, 'shard', split_axis=0, concat_axis=1, tiled=T...]
    unnamed x23 -> x20, local copies, waits for them, and re-layouts: 12.1 us -> 4.16 us
    all_to_all x5 -> x3, local copies, waits for them, and re-layouts: 7.57 us -> 1.12 us  [the longest x1 0.51 us: shards(): lax.all_to_all(send2, 'shard', split_axis=0, concat_axis=0, tiled=True)]
    reshape x0 -> x7, local copies, waits for them, and re-layouts: none -> 5.53 us  [the longest x2 3.43 us: shards(): got2[:, :2 * piece].reshape(owners, 2, own_rows, cols).transpose(1, 0, 2, 3)]
  transfers between devices with their start and end apart: 3 -> 0, of which waited for: 1 -> 0; matrix products, arithmetic and copies ran while one was open for 1% -> 0% of each run, Pallas kernels for 0% -> 0%
where the time goes in v1:
time: 124 us; the launch traced here: 123 us
  blocking collectives  93.6 us (75%)
  local copies, waits for them, and re-layouts  17.2 us (14%)
  other arithmetic  9.04 us (7%)
  between operations  2.97 us (2%)
    all_to_all x1, blocking collectives, shards(): got = lax.all_to_all(send, 'shard', split_axis=0, concat_axis=0, tiled=True)  32.8 us
    all_to_all x1, blocking collectives, rep_sum(): got = lax.all_to_all(pieces, 'rep', split_axis=0, concat_axis=0, tiled=True)  23.5 us
    all_to_all x1, blocking collectives, shards(): lax.all_to_all(send2, 'shard', split_axis=0, concat_axis=0, tiled=True)  20.8 us
    all_to_all x1, blocking collectives, rep_sum(): full = lax.all_to_all(every, 'rep', split_axis=0, concat_axis=0, tiled=True)  16.4 us
    another operation x1, other arithmetic  4.98 us
    unnamed x20, local copies, waits for them, and re-layouts  4.16 us
    reshape x2, local copies, waits for them, and re-layouts, shards(): got2[:, :2 * piece].reshape(owners, 2, own_rows, cols).transpose(1, 0, 2, 3)  3.43 us

profile of v1, /device:TPU:6, one launch (start us, length us, event | category | flops | bytes accessed | tf_op | source)
XLA Modules:
  0.0 122.7 jit_solution(7595264595324059136)
XLA Ops:
  0.6 1.3 %copy.27 = f32[1,1664,64]{2,1,0:T(8,128)S(1)} copy(f32[1,1664,64]{1,2,0:T(8,128)} %param.6) | data formatting | bytes 851968 | tf_op args[0]
  1.9 0.0 copy-start.6
  2.0 0.2 reshape_squeeze.3
  2.1 0.5 copy-done.6
  2.7 0.3 reshape.114
  3.0 0.3 all_to_all.28
  3.3 23.5 %all_to_all.42 = f32[16,1,6784]{2,1,0:T(1,128)S(1)} all-to-all(f32[16,1,6784]{2,1,0:T(1,128)S(1)} %all_to_all.28), channel_id=1, replica_groups=mesh['rep'=16,'shard'=32] {'rep'}, dimensions={0} | all-to-all | bytes 868352 | tf_op jit(solution)/shard_map/all_to_all | solution.py:30
  26.8 0.3 reduce_sum.36
  27.1 0.2 broadcast_in_dim.28
  27.3 16.4 %all_to_all.43 = f32[16,1,6784]{2,1,0:T(1,128)S(1)} all-to-all(f32[16,1,6784]{2,1,0:T(1,128)S(1)} %broadcast_in_dim.28), channel_id=1, replica_groups=mesh['rep'=16,'shard'=32] {'rep'}, dimensions={0} | all-to-all | bytes 868352 | tf_op jit(solution)/shard_map/all_to_all | solution.py:33
  43.7 0.2 reshape.115
  44.0 0.6 fusion.5
  44.6 0.7 multiply_reduce_fusion
  45.3 0.1 reshape_reshape.3
  46.7 0.1 concatenate.29
  46.8 0.3 all_to_all.32
  47.1 32.8 %all_to_all.44 = f32[32,1,3456]{2,1,0:T(1,128)S(1)} all-to-all(f32[32,1,3456]{2,1,0:T(1,128)S(1)} %all_to_all.32), channel_id=1, replica_groups=mesh['rep'=16,'shard'=32] {'shard'}, dimensions={0} | all-to-all | bytes 884736 | tf_op jit(solution)/shard_map/all_to_all | solution.py:60
  79.9 0.6 slice_reduce_fusion.1
  81.3 0.3 reshape.116
  81.6 0.0 copy-start.5
  81.6 0.2 copy.28
  81.8 0.0 copy-start.3
  81.8 0.0 copy-start.4
  81.8 0.5 concatenate.30
  82.3 0.3 copy-done.5
  82.6 0.2 copy-done.3
  82.8 0.1 copy-done.4
  82.9 5.0 %fusion.3 = (bf16[1,106896]{1,0:T(2,128)(2,1)S(1)}, f32[1,106896]{1,0:T(1,128)S(1)}, f32[1,106896]{1,0:T(1,128)}, f32[1,106896]{1,0:T(1,128)}) fusion(f32[1,106896]{1,0:T(1,128)S(1)} %copy-done.3, f32[]{:T(128)S(6)} %mul.88, f32[1,400]{1,0:T(1,128)S(1)} %bitcast.29, f32[1,106496]{1,0:T(1,128)S(1)} %concatenate.30, f32[1,106896]{1,0:T(1,128)S(1)} %copy-done.4, ...), kind=kLoop, calls=%fused_computation.20 | loop fusion | flops 2137920 | bytes 3206884 | tf_op jit(solution)/shard_map/convert.2
  87.9 0.0 copy-start
  87.9 1.2 slice_reduce_fusion
  89.1 0.2 stack.9
  89.3 0.0 copy-start.2
  89.4 0.2 copy.29
  89.5 0.0 copy-done
  89.5 0.8 copy-done.2
  90.4 0.7 multiply_add_fusion
  91.1 0.0 copy-start.1
  91.1 1.1 fusion.2
  92.2 0.2 stack.10
  92.4 0.0 copy-done.1
  92.5 0.2 copy.30
  92.6 0.2 maximum_bitcast_fusion
  92.8 0.6 reshape.117
  93.4 0.1 concatenate.33
  93.5 0.5 broadcast.70
  94.0 0.9 reduce.9
  95.0 0.3 reshape.124
  95.3 20.8 %all_to_all.45 = bf16[32,2,3584]{2,1,0:T(2,128)(2,1)S(1)} all-to-all(bf16[32,2,3584]{2,1,0:T(2,128)(2,1)S(1)} %reshape.124), channel_id=1, replica_groups=mesh['rep'=16,'shard'=32] {'shard'}, dimensions={0} | all-to-all | bytes 917504 | tf_op jit(solution)/shard_map/all_to_all | solution.py:93
  116.1 0.4 reshape.125
  116.5 0.2 copy.39
  116.7 0.7 reshape.120
  117.5 0.8 reshape.118
  118.2 1.8 %copy.32 = bf16[2,32,52,64]{2,1,3,0:T(8,128)(2,1)S(1)} copy(bf16[2,32,52,64]{3,2,0,1:T(8,128)(2,1)S(1)} %bitcast.22) | data formatting | bytes 851968 | tf_op jit(solution)/shard_map/transpose | solution.py:95
  120.1 2.7 %reshape.119 = bf16[2,1664,64]{1,2,0:T(8,128)(2,1)} reshape(bf16[2,32,52,64]{2,1,3,0:T(8,128)(2,1)S(1)} %copy.32) | data formatting | bytes 851968 | tf_op jit(solution)/shard_map/reshape | solution.py:95
  (12 shorter events, 0.2 us)
Async XLA Ops:
  1.9 0.7 copy-start.6
  81.6 1.0 copy-start.5
  81.8 1.0 copy-start.3
  81.8 1.2 copy-start.4
  87.9 1.6 %copy-start = (f32[1,106896]{1,0:T(1,128)}, f32[1,106896]{1,0:T(1,128)S(1)}, u32[]{:S(2)}) copy-start(f32[1,106896]{1,0:T(1,128)S(1)} %get-tuple-element.7) | copy-start | bytes 1282756
  89.3 1.0 copy-start.2
  91.1 1.3 %copy-start.1 = (f32[1,106896]{1,0:T(1,128)}, f32[1,106896]{1,0:T(1,128)S(1)}, u32[]{:S(2)}) copy-start(f32[1,106896]{1,0:T(1,128)S(1)} %multiply_add_fusion) | copy-start | bytes 1282756

commit v2 on v1

--- a/solution.py
+++ b/solution.py
@@ -22,44 +22,46 @@
     return -(-n // LANE) * LANE
 
 
-def rep_sum(flat, replicas):
-    n = flat.shape[0]
-    chunk = n // replicas
-    width = _pad_to(chunk)
-    pieces = jnp.pad(flat.reshape(replicas, chunk), ((0, 0), (0, width - chunk)))
-    got = lax.all_to_all(pieces, "rep", split_axis=0, concat_axis=0, tiled=True)
-    mine = jnp.sum(got, axis=0)
-    every = jnp.broadcast_to(mine[None], (replicas, width))
-    full = lax.all_to_all(every, "rep", split_axis=0, concat_axis=0, tiled=True)
-    return full[:, :chunk].reshape(n)
-
-
 def shards(grad_blocks, gain_grads, first_moment, second_moment, master_flat, ema_flat):
     replicas = lax.axis_size("rep")
     owners = lax.axis_size("shard")
+    me = lax.axis_index("shard")
     rows, cols = grad_blocks.shape[1], grad_blocks.shape[2]
     small = gain_grads.shape[1]
-    main_block = rows * cols
-    flat = jnp.concatenate([grad_blocks[0].reshape(main_block), gain_grads[0]])
-    summed = rep_sum(flat, replicas)
-    matrix_part = summed[:main_block].reshape(rows, cols)
-    small_part = summed[main_block:]
-    partial_value = jnp.sum(matrix_part * matrix_part) + jnp.sum(small_part * small_part)
-
     own_rows = rows // owners
     piece = own_rows * cols
-    width = _pad_to(piece + 1)
+    sub = piece // replicas
+    gsub = small // replicas
+    block = grad_blocks[0].reshape(owners, replicas, sub).transpose(1, 0, 2).reshape(replicas, owners * sub)
+    gains_in = gain_grads[0].reshape(replicas, gsub)
+    width = _pad_to(owners * sub + gsub)
     send = jnp.concatenate(
+        [block, gains_in, jnp.zeros((replicas, width - owners * sub - gsub), jnp.float32)], axis=1
+    )
+    got = lax.all_to_all(send, "rep", split_axis=0, concat_axis=0, tiled=True)
+    mine = jnp.sum(got, axis=0)
+    chunk = mine[: owners * sub].reshape(owners, sub)
+    gain_chunk = mine[owners * sub : owners * sub + gsub]
+    partial_value = jnp.sum(chunk * chunk) + jnp.sum(gain_chunk * gain_chunk)
+    width2 = _pad_to(sub + gsub + 1)
+    rowdata = jnp.concatenate(
         [
-            matrix_part.reshape(owners, piece),
+            chunk,
+            jnp.broadcast_to(gain_chunk[None], (owners, gsub)),
             jnp.broadcast_to(partial_value, (owners, 1)),
-            jnp.zeros((owners, width - piece - 1), jnp.float32),
+            jnp.zeros((owners, width2 - sub - gsub - 1), jnp.float32),
         ],
         axis=1,
     )
-    got = lax.all_to_all(send, "shard", split_axis=0, concat_axis=0, tiled=True)
-    total = jnp.sum(got[:, piece]) / (replicas * replicas)
-    owned = got[:, :piece].reshape(owners, own_rows, cols).transpose(1, 0, 2)
+    send2 = jnp.broadcast_to(rowdata[None], (replicas, owners, width2)).reshape(replicas * owners, width2)
+    got2 = lax.all_to_all(send2, ("rep", "shard"), split_axis=0, concat_axis=0, tiled=True)
+    got2 = got2.reshape(replicas, owners, width2)
+    total = jnp.sum(got2[:, :, sub + gsub]) / (replicas * replicas)
+    owned = (
+        got2[:, :, :sub].transpose(1, 0, 2).reshape(owners, own_rows, cols).transpose(1, 0, 2)
+    )
+    small_part = lax.dynamic_index_in_dim(got2[:, :, sub : sub + gsub], me, axis=1, keepdims=False)
+    small_part = small_part.reshape(small)
     main_len = own_rows * owners * cols
     grads = jnp.concatenate([owned.reshape(main_len), small_part]).reshape(1, -1) / replicas
     rms = jnp.sqrt(total / PARAMS)

time: 124 us -> 119 us (0.960)
  blocking collectives: 93.6 us -> 20 us
  waiting for transfers between devices: 0 us -> 34.3 us
  starting transfers between devices: 0 us -> 28.6 us
  local copies, waits for them, and re-layouts: 17.2 us -> 20.4 us
  other arithmetic: 9.04 us -> 10.4 us
    all_to_all x3 -> x0, blocking collectives: 72.7 us -> none  [the longest x1 32.8 us: shards(): got = lax.all_to_all(send, 'shard', split_axis=0, concat_axis=0, tiled=True)]
    all_to_all x0 -> x2, waiting for transfers between devices: none -> 34.3 us  [the longest x1 20.7 us: shards(): lax.all_to_all(send2, ('rep', 'shard'), split_axis=0, concat_axis=0, tile...]
    all_to_all x0 -> x2, starting transfers between devices: none -> 28.6 us  [the longest x1 18.5 us: shards(): lax.all_to_all(send2, ('rep', 'shard'), split_axis=0, concat_axis=0, tile...]
    all_to_all x2, local copies, waits for them, and re-layouts: 0.6 us -> 2.54 us  [the longest x1 1.32 us: shards(): lax.all_to_all(send2, ('rep', 'shard'), split_axis=0, concat_axis=0, tile...]
    unnamed x0 -> x1, other arithmetic: none -> 1.34 us
    unnamed x20 -> x18, local copies, waits for them, and re-layouts: 4.16 us -> 4.15 us
  transfers between devices with their start and end apart: 0 -> 2, of which waited for: 0 -> 2; matrix products, arithmetic and copies ran while one was open for 0% -> 0% of each run, Pallas kernels for 0% -> 0%
where the time goes in v2:
time: 119 us; the launch traced here: 117 us
  waiting for transfers between devices  34.3 us (29%)
  starting transfers between devices  28.6 us (24%)
  local copies, waits for them, and re-layouts  20.4 us (17%)
  blocking collectives  20 us (17%)
  other arithmetic  10.4 us (9%)
  between operations  2.99 us (3%)
    all_to_all x1, waiting for transfers between devices, shards(): lax.all_to_all(send2, ('rep', 'shard'), split_axis=0, concat_axis=0, tile...  20.7 us
    all_to_all x1, blocking collectives, shards(): lax.all_to_all(send2, 'shard', split_axis=0, concat_axis=0, tiled=True)  20 us
    all_to_all x1, starting transfers between devices, shards(): lax.all_to_all(send2, ('rep', 'shard'), split_axis=0, concat_axis=0, tile...  18.5 us
    all_to_all x1, waiting for transfers between devices, shards(): got = lax.all_to_all(send, 'rep', split_axis=0, concat_axis=0, tiled=True)  13.6 us
    all_to_all x1, starting transfers between devices, shards(): got = lax.all_to_all(send, 'rep', split_axis=0, concat_axis=0, tiled=True)  10.1 us
    another operation x1, other arithmetic  4.98 us
    unnamed x18, local copies, waits for them, and re-layouts  4.15 us
    reshape x2, local copies, waits for them, and re-layouts, shards(): got2[:, :2 * piece].reshape(owners, 2, own_rows, cols).transpose(1, 0, 2, 3)  3.43 us
  transfers between devices with their start and end apart: 2, of which 2 were waited for; matrix products, arithmetic and copies ran while one was open for 0% of the time, Pallas kernels for 0%

profile of v2, /device:TPU:6, one launch (start us, length us, event | category | flops | bytes accessed | tf_op | source)
XLA Modules:
  0.0 116.7 jit_solution(16714046611916130412)
XLA Ops:
  0.6 0.5 broadcast.75
  1.1 1.3 %reduce.16 = f32[400]{0:T(512)S(1)} reduce(f32[1,400]{1,0:T(1,128)} %param.7, f32[]{:T(128)} %broadcast.75), dimensions={0}, to_apply=%param.7.reduce_sub_computation.3 | reduce | bytes 3204 | tf_op args[1]
  2.5 0.1 reshape_squeeze.7
  2.6 1.3 %copy.35 = f32[1,1664,64]{2,1,0:T(8,128)S(1)} copy(f32[1,1664,64]{1,2,0:T(8,128)} %param.6) | data formatting | bytes 851968 | tf_op args[0]
  3.9 0.4 reshape_squeeze.6
  4.3 0.3 copy.36
  4.6 0.3 reshape.122
  4.9 0.1 concatenate.28
  5.0 1.2 %copy.37 = f32[16,1,6784]{2,1,0:T(1,128)} copy(f32[16,1,6784]{2,0,1:T(8,128)S(1)} %bitcast.27) | data formatting | bytes 868352 | tf_op jit(solution)/shard_map/all_to_all | solution.py:41
  6.2 10.1 %all-to-all-start = ((f32[16,1,6784]{2,1,0:T(1,128)}), f32[16,1,6784]{2,1,0:T(1,128)S(1)}, u32[]{:S(2)}, u32[]{:S(2)}) async-start(f32[16,1,6784]{2,1,0:T(1,128)} %copy.37), calls=%async_computation | async-start | bytes 868352 | tf_op jit(solution)/shard_map/all_to_all | solution.py:41
  16.3 0.1 pad.7.clone
  16.3 13.6 %all-to-all-done = f32[16,1,6784]{2,1,0:T(1,128)S(1)} async-done(((f32[16,1,6784]{2,1,0:T(1,128)}), f32[16,1,6784]{2,1,0:T(1,128)S(1)}, u32[]{:S(2)}, u32[]{:S(2)}) %all-to-all-start) | async-done | bytes 434208 | tf_op jit(solution)/shard_map/all_to_all | solution.py:41
  29.9 0.3 reduce_sum.36
  30.2 0.6 fusion.5
  30.8 0.6 multiply_reduce_fusion
  31.4 0.1 pad.5.clone
  32.8 0.1 pad.6.clone
  32.9 0.1 reshape.123
  33.0 1.3 %all_to_all.22 = f32[512,1,256]{2,1,0:T(1,128)} reshape(f32[16,32,256]{2,1,0:T(8,128)S(1)} %broadcast_in_dim.41) | data formatting | bytes 1048576 | tf_op jit(solution)/shard_map/all_to_all | solution.py:57
  34.3 18.5 %all-to-all-start.1 = ((f32[512,1,256]{2,1,0:T(1,128)}), f32[512,1,256]{2,1,0:T(1,128)S(1)}, u32[]{:S(2)}, u32[]{:S(2)}) async-start(f32[512,1,256]{2,1,0:T(1,128)} %all_to_all.22), calls=%async_computation.1 | async-start | bytes 1048576 | tf_op jit(solution)/shard_map/all_to_all | solution.py:57
  52.9 20.7 %all-to-all-done.1 = f32[512,1,256]{2,1,0:T(1,128)S(1)} async-done(((f32[512,1,256]{2,1,0:T(1,128)}), f32[512,1,256]{2,1,0:T(1,128)S(1)}, u32[]{:S(2)}, u32[]{:S(2)}) %all-to-all-start.1) | async-done | bytes 524320 | tf_op jit(solution)/shard_map/all_to_all | solution.py:57
  73.6 0.7 slice_reduce_fusion.1
  74.4 0.1 slice.46
  75.3 0.1 concatenate.31
  75.4 0.3 copy.38
  75.7 0.6 reshape.125
  76.4 0.0 copy-start.5
  76.4 0.2 copy.39
  76.6 0.0 copy-start.3
  76.6 0.0 copy-start.4
  76.6 0.5 concatenate.30
  77.2 0.3 copy-done.5
  77.4 0.2 copy-done.3
  77.6 0.1 copy-done.4
  77.8 5.0 %fusion.3 = (bf16[1,106896]{1,0:T(2,128)(2,1)S(1)}, f32[1,106896]{1,0:T(1,128)S(1)}, f32[1,106896]{1,0:T(1,128)}, f32[1,106896]{1,0:T(1,128)}) fusion(f32[1,106896]{1,0:T(1,128)S(1)} %copy-done.3, f32[]{:T(128)S(6)} %mul.88, f32[1,400]{1,0:T(1,128)S(1)} %concatenate.31, f32[1,106496]{1,0:T(1,128)S(1)} %concatenate.30, f32[1,106896]{1,0:T(1,128)S(1)} %copy-done.4, ...), kind=kLoop, calls=%fused_computation.20 | loop fusion | flops 2137920 | bytes 3206884 | tf_op jit(solution)/shard_map/convert.2
  82.7 0.0 copy-start
  82.8 1.2 %slice_reduce_fusion = bf16[106496]{0:T(1024)(128)(2,1)S(1)} fusion(bf16[1,106896]{1,0:T(2,128)(2,1)S(1)} %get-tuple-element.6), kind=kLoop, calls=%fused_computation.13 | loop fusion | bytes 425984 | tf_op jit(solution)/shard_map/slice | solution.py:81
  84.0 0.2 stack.9
  84.2 0.0 copy-start.2
  84.2 0.2 copy.40
  84.4 0.0 copy-done
  84.4 0.8 copy-done.2
  85.2 0.7 multiply_add_fusion
  85.9 0.0 copy-start.1
  85.9 1.1 fusion.2
  87.1 0.2 stack.10
  87.3 0.0 copy-done.1
  87.3 0.2 copy.41
  87.5 0.2 maximum_bitcast_fusion
  87.7 0.6 reshape.126
  88.3 0.1 concatenate.33
  88.4 0.5 broadcast.80
  88.9 0.9 reduce.17
  89.8 0.3 reshape.149
  90.1 20.0 %all_to_all.30 = bf16[32,2,3584]{2,1,0:T(2,128)(2,1)S(1)} all-to-all(bf16[32,2,3584]{2,1,0:T(2,128)(2,1)S(1)} %reshape.149), channel_id=1, replica_groups=mesh['rep'=16,'shard'=32] {'shard'}, dimensions={0} | all-to-all | bytes 917504 | tf_op jit(solution)/shard_map/all_to_all | solution.py:95
  110.1 0.4 reshape.150
  110.5 0.2 copy.47
  110.7 0.7 reshape.129
  111.4 0.8 reshape.127
  112.2 1.8 %copy.43 = bf16[2,32,52,64]{2,1,3,0:T(8,128)(2,1)S(1)} copy(bf16[2,32,52,64]{3,2,0,1:T(8,128)(2,1)S(1)} %bitcast.22) | data formatting | bytes 851968 | tf_op jit(solution)/shard_map/transpose | solution.py:97
  114.0 2.7 %reshape.128 = bf16[2,1664,64]{1,2,0:T(8,128)(2,1)} reshape(bf16[2,32,52,64]{2,1,3,0:T(8,128)(2,1)S(1)} %copy.43) | data formatting | bytes 851968 | tf_op jit(solution)/shard_map/reshape | solution.py:97
  (12 shorter events, 0.2 us)
Async XLA Ops:
  6.2 23.7 %all-to-all-start = ((f32[16,1,6784]{2,1,0:T(1,128)}), f32[16,1,6784]{2,1,0:T(1,128)S(1)}, u32[]{:S(2)}, u32[]{:S(2)}) async-start(f32[16,1,6784]{2,1,0:T(1,128)} %copy.37), calls=%async_computation | async-start | bytes 868352 | tf_op jit(solution)/shard_map/all_to_all | solution.py:41
  34.3 39.3 %all-to-all-start.1 = ((f32[512,1,256]{2,1,0:T(1,128)}), f32[512,1,256]{2,1,0:T(1,128)S(1)}, u32[]{:S(2)}, u32[]{:S(2)}) async-start(f32[512,1,256]{2,1,0:T(1,128)} %all_to_all.22), calls=%async_computation.1 | async-start | bytes 1048576 | tf_op jit(solution)/shard_map/all_to_all | solution.py:57
  76.4 1.0 copy-start.5
  76.6 1.0 copy-start.3
  76.6 1.2 copy-start.4
  82.7 1.6 %copy-start = (f32[1,106896]{1,0:T(1,128)}, f32[1,106896]{1,0:T(1,128)S(1)}, u32[]{:S(2)}) copy-start(f32[1,106896]{1,0:T(1,128)S(1)} %get-tuple-element.7) | copy-start | bytes 1282756
  84.2 1.0 copy-start.2
  85.9 1.3 %copy-start.1 = (f32[1,106896]{1,0:T(1,128)}, f32[1,106896]{1,0:T(1,128)S(1)}, u32[]{:S(2)}) copy-start(f32[1,106896]{1,0:T(1,128)S(1)} %multiply_add_fusion) | copy-start | bytes 1282756

commit v3 on v1

--- a/solution.py
+++ b/solution.py
@@ -1,6 +1,10 @@
 import jax
 import jax.numpy as jnp
 from jax import lax
+import functools
+
+from jax.experimental import pallas as pl
+from jax.experimental.pallas import tpu as pltpu
 from jax.sharding import PartitionSpec as P
 
 STEP = 100
@@ -16,10 +20,82 @@
 clip_eps = 1e-06
 
 LANE = 128
+TILE = {jnp.dtype(jnp.float32): 8 * LANE, jnp.dtype(jnp.bfloat16): 16 * LANE}
 
 
-def _pad_to(n):
-    return -(-n // LANE) * LANE
+def _pad_to(n, dtype=jnp.float32):
+    unit = TILE[jnp.dtype(dtype)]
+    return -(-n // unit) * unit
+
+
+MESH = pl.DeviceIdType.MESH
+
+
+def _a2a_kernel(axis, other_axis, n, x_ref, y_ref, send_sem, recv_sem, local_sem):
+    me = lax.axis_index(axis)
+    other = lax.axis_index(other_axis)
+
+    def dev(j):
+        return (other, j) if axis == "shard" else (j, other)
+
+    barrier = pltpu.get_barrier_semaphore()
+    for k in range(1, n):
+        pl.semaphore_signal(barrier, inc=1, device_id=dev(lax.rem(me + k, n)), device_id_type=MESH)
+    pl.semaphore_wait(barrier, n - 1)
+    local = pltpu.make_async_copy(x_ref.at[me], y_ref.at[me], local_sem)
+    local.start()
+    for k in range(1, n):
+        j = lax.rem(me + k, n)
+        pltpu.make_async_remote_copy(
+            src_ref=x_ref.at[j],
+            dst_ref=y_ref.at[me],
+            send_sem=send_sem.at[k],
+            recv_sem=recv_sem.at[k],
+            device_id=dev(j),
+            device_id_type=MESH,
+        ).start()
+    local.wait()
+    for k in range(1, n):
+        j = lax.rem(me + k, n)
+        src = lax.rem(me + n - k, n)
+        pltpu.make_async_remote_copy(
+            src_ref=x_ref.at[j],
+            dst_ref=y_ref.at[src],
+            send_sem=send_sem.at[k],
+            recv_sem=recv_sem.at[k],
+            device_id=dev(j),
+            device_id_type=MESH,
+        ).wait_send()
+        pltpu.make_async_remote_copy(
+            src_ref=x_ref.at[j],
+            dst_ref=y_ref.at[src],
+            send_sem=send_sem.at[k],
+            recv_sem=recv_sem.at[k],
+            device_id=dev(j),
+            device_id_type=MESH,
+        ).wait_recv()
+
+
+def all_to_all(x, axis, other_axis, n, collective_id):
+    return pl.pallas_call(
+        functools.partial(_a2a_kernel, axis, other_axis, n),
+        out_shape=jax.ShapeDtypeStruct(x.shape, x.dtype),
+        in_specs=[pl.BlockSpec(memory_space=pl.ANY)],
+        out_specs=pl.BlockSpec(memory_space=pl.ANY),
+        scratch_shapes=[
+            pltpu.SemaphoreType.DMA((n,)),
+            pltpu.SemaphoreType.DMA((n,)),
+            pltpu.SemaphoreType.DMA,
+        ],
+        compiler_params=pltpu.CompilerParams(collective_id=collective_id, has_side_effects=True),
+    )(x)
+
+
+def exchange(pieces, axis, collective_id):
+    other = "rep" if axis == "shard" else "shard"
+    n, width = pieces.shape
+    got = all_to_all(pieces.reshape(n, width // LANE, LANE), axis, other, n, collective_id)
+    return got.reshape(n, width)
 
 
 def rep_sum(flat, replicas):
@@ -27,10 +103,10 @@
     chunk = n // replicas
     width = _pad_to(chunk)
     pieces = jnp.pad(flat.reshape(replicas, chunk), ((0, 0), (0, width - chunk)))
-    got = lax.all_to_all(pieces, "rep", split_axis=0, concat_axis=0, tiled=True)
+    got = exchange(pieces, "rep", 0)
     mine = jnp.sum(got, axis=0)
     every = jnp.broadcast_to(mine[None], (replicas, width))
-    full = lax.all_to_all(every, "rep", split_axis=0, concat_axis=0, tiled=True)
+    full = exchange(every, "rep", 1)
     return full[:, :chunk].reshape(n)
 
 
@@ -57,7 +133,7 @@
         ],
         axis=1,
     )
-    got = lax.all_to_all(send, "shard", split_axis=0, concat_axis=0, tiled=True)
+    got = exchange(send, "shard", 2)
     total = jnp.sum(got[:, piece]) / (replicas * replicas)
     owned = got[:, :piece].reshape(owners, own_rows, cols).transpose(1, 0, 2)
     main_len = own_rows * owners * cols
@@ -81,7 +157,7 @@
     stacked = jnp.stack([weights, averaged], axis=0).reshape(2, own_rows, owners, cols)
     back = stacked.transpose(2, 0, 1, 3).reshape(owners, 2 * piece)
     gains_mine = new_master[0, main_len:].astype(jnp.bfloat16)
-    width2 = _pad_to(2 * piece + small)
+    width2 = _pad_to(2 * piece + small, jnp.bfloat16)
     send2 = jnp.concatenate(
         [
             back,
@@ -90,7 +166,7 @@
         ],
         axis=1,
     )
-    got2 = lax.all_to_all(send2, "shard", split_axis=0, concat_axis=0, tiled=True)
+    got2 = exchange(send2, "shard", 3)
     weight_blocks = (
         got2[:, : 2 * piece].reshape(owners, 2, own_rows, cols).transpose(1, 0, 2, 3).reshape(2, rows, cols)
     )

time: 124 us -> 125 us (level)
  blocking collectives: 93.6 us -> 0 us
  Pallas kernels: 0 us -> 90.1 us
  local copies, waits for them, and re-layouts: 17.2 us -> 22.5 us
    all_to_all x4 -> x0, blocking collectives: 93.6 us -> none  [the longest x1 32.8 us: shards(): got = lax.all_to_all(send, 'shard', split_axis=0, concat_axis=0, tiled=True)]
    pallas_call x0 -> x4, Pallas kernels: none -> 90.1 us  [all_to_all(): pl.pallas_call(functools.partial(_a2a_kernel, axis, other_axis, n), out_s...]
    unnamed x20 -> x22, local copies, waits for them, and re-layouts: 4.16 us -> 9.79 us
where the time goes in v3:
time: 125 us; the launch traced here: 124 us
  Pallas kernels  90.1 us (72%)
  local copies, waits for them, and re-layouts  22.5 us (18%)
  other arithmetic  8.91 us (7%)
  between operations  2.98 us (2%)
    pallas_call x4, Pallas kernels, all_to_all(): pl.pallas_call(functools.partial(_a2a_kernel, axis, other_axis, n), out_s...  90.1 us
    unnamed x22, local copies, waits for them, and re-layouts  9.79 us
    another operation x1, other arithmetic  4.98 us
    reshape x2, local copies, waits for them, and re-layouts, shards(): got2[:, :2 * piece].reshape(owners, 2, own_rows, cols).transpose(1, 0, 2, 3)  3.43 us

profile of v3, /device:TPU:6, one launch (start us, length us, event | category | flops | bytes accessed | tf_op | source)
XLA Modules:
  0.0 124.5 jit_solution(17477156967245681721)
XLA Ops:
  0.6 1.3 %copy.19 = f32[1,1664,64]{2,1,0:T(8,128)S(1)} copy(f32[1,1664,64]{1,2,0:T(8,128)} %param.6) | data formatting | bytes 851968 | tf_op args[0]
  1.9 0.0 copy-start.6
  2.0 0.2 reshape_squeeze.3
  2.1 0.5 copy-done.6
  2.7 0.3 reshape.128
  3.0 0.9 copy.24
  3.8 24.1 %shard_map.109 = f32[16,56,128]{2,1,0:T(8,128)} custom-call(f32[16,56,128]{2,1,0:T(8,128)} %bitcast.39), custom_call_target="tpu_custom_call" | custom-call | tf_op jit(solution)/shard_map/pallas_call | solution.py:80
  28.0 1.1 reduce_sum.36
  29.0 0.8 broadcast_in_dim.28.x_ref
  29.8 16.5 %shard_map.110 = f32[16,56,128]{2,1,0:T(8,128)} custom-call(f32[16,56,128]{2,1,0:T(8,128)} %broadcast_in_dim.28.x_ref), custom_call_target="tpu_custom_call" | custom-call | tf_op jit(solution)/shard_map/pallas_call | solution.py:80
  46.3 1.1 copy.35
  47.5 0.2 reshape.131
  47.7 0.6 fusion.5
  48.3 0.7 multiply_reduce_fusion
  50.3 0.1 reshape_reshape.3
  50.4 0.1 concatenate.29
  50.6 0.9 copy.26
  51.4 27.8 %shard_map.111 = f32[32,32,128]{2,1,0:T(8,128)} custom-call(f32[32,32,128]{2,1,0:T(8,128)} %bitcast.33), custom_call_target="tpu_custom_call" | custom-call | tf_op jit(solution)/shard_map/pallas_call | solution.py:80
  79.3 1.3 %copy.34 = f32[4,8,32,128]{3,1,2,0:T(8,128)S(1)} copy(f32[4,8,32,128]{3,2,1,0:T(8,128)} %bitcast.34) | data formatting | bytes 1048576
  80.6 0.6 slice_reduce_fusion.1
  82.0 0.3 reshape.134
  82.3 0.0 copy-start.5
  82.3 0.2 copy.20
  82.5 0.0 copy-start.3
  82.5 0.0 copy-start.4
  82.5 0.5 concatenate.30
  83.0 0.3 copy-done.5
  83.3 0.2 copy-done.3
  83.5 0.1 copy-done.4
  83.6 5.0 %fusion.3 = (bf16[1,106896]{1,0:T(2,128)(2,1)S(1)}, f32[1,106896]{1,0:T(1,128)S(1)}, f32[1,106896]{1,0:T(1,128)}, f32[1,106896]{1,0:T(1,128)}) fusion(f32[1,106896]{1,0:T(1,128)S(1)} %copy-done.3, f32[]{:T(128)S(6)} %mul.88, f32[1,400]{1,0:T(1,128)S(1)} %bitcast.44, f32[1,106496]{1,0:T(1,128)S(1)} %concatenate.30, f32[1,106896]{1,0:T(1,128)S(1)} %copy-done.4, ...), kind=kLoop, calls=%fused_computation.21 | loop fusion | flops 2137920 | bytes 3206884 | tf_op jit(solution)/shard_map/convert.2
  88.6 0.0 copy-start
  88.7 1.2 slice_reduce_fusion
  89.9 0.2 stack.9
  90.1 0.0 copy-start.2
  90.1 0.2 copy.21
  90.3 0.0 copy-done
  90.3 0.8 copy-done.2
  91.1 0.7 multiply_add_fusion
  91.8 0.0 copy-start.1
  91.8 1.1 fusion.2
  93.0 0.2 stack.10
  93.2 0.0 copy-done.1
  93.2 0.2 copy.22
  93.4 0.2 maximum_bitcast_fusion
  93.6 0.6 reshape.135
  94.2 0.3 concatenate.33
  94.4 0.9 copy.28
  95.4 21.6 %shard_map.112 = bf16[32,64,128]{2,1,0:T(8,128)(2,1)} custom-call(bf16[32,64,128]{2,1,0:T(8,128)(2,1)} %bitcast.35), custom_call_target="tpu_custom_call" | custom-call | tf_op jit(solution)/shard_map/pallas_call | solution.py:80
  117.0 1.4 %copy.33 = bf16[4,8,64,128]{3,1,2,0:T(8,128)(2,1)S(1)} copy(bf16[4,8,64,128]{3,2,1,0:T(8,128)(2,1)} %bitcast.36) | data formatting | bytes 1048576
  118.4 0.7 reshape.140
  119.2 0.8 reshape.138
  119.9 1.8 %copy.23 = bf16[2,32,52,64]{2,1,3,0:T(8,128)(2,1)S(1)} copy(bf16[2,32,52,64]{3,2,0,1:T(8,128)(2,1)S(1)} %bitcast.30) | data formatting | bytes 851968 | tf_op jit(solution)/shard_map/transpose | solution.py:171
  121.8 2.7 %reshape.139 = bf16[2,1664,64]{1,2,0:T(8,128)(2,1)} reshape(bf16[2,32,52,64]{2,1,3,0:T(8,128)(2,1)S(1)} %copy.23) | data formatting | bytes 851968 | tf_op jit(solution)/shard_map/reshape | solution.py:171
  (11 shorter events, 0.2 us)
Async XLA Ops:
  1.9 0.7 copy-start.6
  82.3 1.0 copy-start.5
  82.5 1.0 copy-start.3
  82.5 1.2 copy-start.4
  88.6 1.6 %copy-start = (f32[1,106896]{1,0:T(1,128)}, f32[1,106896]{1,0:T(1,128)S(1)}, u32[]{:S(2)}) copy-start(f32[1,106896]{1,0:T(1,128)S(1)} %get-tuple-element.7) | copy-start | bytes 1282756
  90.1 1.0 copy-start.2
  91.8 1.3 %copy-start.1 = (f32[1,106896]{1,0:T(1,128)}, f32[1,106896]{1,0:T(1,128)S(1)}, u32[]{:S(2)}) copy-start(f32[1,106896]{1,0:T(1,128)S(1)} %multiply_add_fusion) | copy-start | bytes 1282756

commit v4 on v3

--- a/solution.py
+++ b/solution.py
@@ -31,24 +31,27 @@
 MESH = pl.DeviceIdType.MESH
 
 
-def _a2a_kernel(axis, other_axis, n, x_ref, y_ref, send_sem, recv_sem, local_sem):
+def _a2a_kernel(axis, other_axis, stride, n, x_ref, y_ref, send_sem, recv_sem, local_sem):
     me = lax.axis_index(axis)
     other = lax.axis_index(other_axis)
+    pos = lax.rem(lax.div(me, stride), n)
+    base = me - pos * stride
 
     def dev(j):
-        return (other, j) if axis == "shard" else (j, other)
+        index = base + j * stride
+        return (other, index) if axis == "shard" else (index, other)
 
     barrier = pltpu.get_barrier_semaphore()
     for k in range(1, n):
-        pl.semaphore_signal(barrier, inc=1, device_id=dev(lax.rem(me + k, n)), device_id_type=MESH)
+        pl.semaphore_signal(barrier, inc=1, device_id=dev(lax.rem(pos + k, n)), device_id_type=MESH)
     pl.semaphore_wait(barrier, n - 1)
-    local = pltpu.make_async_copy(x_ref.at[me], y_ref.at[me], local_sem)
+    local = pltpu.make_async_copy(x_ref.at[pos], y_ref.at[pos], local_sem)
     local.start()
     for k in range(1, n):
-        j = lax.rem(me + k, n)
+        j = lax.rem(pos + k, n)
         pltpu.make_async_remote_copy(
             src_ref=x_ref.at[j],
-            dst_ref=y_ref.at[me],
+            dst_ref=y_ref.at[pos],
             send_sem=send_sem.at[k],
             recv_sem=recv_sem.at[k],
             device_id=dev(j),
@@ -56,29 +59,24 @@
         ).start()
     local.wait()
     for k in range(1, n):
-        j = lax.rem(me + k, n)
-        src = lax.rem(me + n - k, n)
-        pltpu.make_async_remote_copy(
+        j = lax.rem(pos + k, n)
+        src = lax.rem(pos + n - k, n)
+        copy = pltpu.make_async_remote_copy(
             src_ref=x_ref.at[j],
             dst_ref=y_ref.at[src],
             send_sem=send_sem.at[k],
             recv_sem=recv_sem.at[k],
             device_id=dev(j),
             device_id_type=MESH,
-        ).wait_send()
-        pltpu.make_async_remote_copy(
-            src_ref=x_ref.at[j],
-            dst_ref=y_ref.at[src],
-            send_sem=send_sem.at[k],
-            recv_sem=recv_sem.at[k],
-            device_id=dev(j),
-            device_id_type=MESH,
-        ).wait_recv()
+        )
+        copy.wait_send()
+        copy.wait_recv()
 
 
-def all_to_all(x, axis, other_axis, n, collective_id):
+def all_to_all(x, axis, other_axis, stride, collective_id):
+    n = x.shape[0]
     return pl.pallas_call(
-        functools.partial(_a2a_kernel, axis, other_axis, n),
+        functools.partial(_a2a_kernel, axis, other_axis, stride, n),
         out_shape=jax.ShapeDtypeStruct(x.shape, x.dtype),
         in_specs=[pl.BlockSpec(memory_space=pl.ANY)],
         out_specs=pl.BlockSpec(memory_space=pl.ANY),
@@ -91,23 +89,25 @@
     )(x)
 
 
-def exchange(pieces, axis, collective_id):
+def exchange(pieces, axis, collective_id, stride=1):
     other = "rep" if axis == "shard" else "shard"
     n, width = pieces.shape
-    got = all_to_all(pieces.reshape(n, width // LANE, LANE), axis, other, n, collective_id)
+    got = all_to_all(pieces.reshape(n, width // LANE, LANE), axis, other, stride, collective_id)
     return got.reshape(n, width)
 
 
 def rep_sum(flat, replicas):
+    cores = 2
+    chips = replicas // cores
     n = flat.shape[0]
-    chunk = n // replicas
-    width = _pad_to(chunk)
-    pieces = jnp.pad(flat.reshape(replicas, chunk), ((0, 0), (0, width - chunk)))
-    got = exchange(pieces, "rep", 0)
-    mine = jnp.sum(got, axis=0)
-    every = jnp.broadcast_to(mine[None], (replicas, width))
-    full = exchange(every, "rep", 1)
-    return full[:, :chunk].reshape(n)
+    quarter = -(-n // replicas)
+    width = _pad_to(quarter)
+    padded = jnp.pad(flat, (0, width * replicas - n)).reshape(cores, chips * width)
+    half = jnp.sum(exchange(padded, "rep", 0, 1), axis=0)
+    mine = jnp.sum(exchange(half.reshape(chips, width), "rep", 1, cores), axis=0)
+    every = exchange(jnp.broadcast_to(mine[None], (chips, width)), "rep", 4, cores)
+    whole = exchange(jnp.broadcast_to(every.reshape(1, chips * width), (cores, chips * width)), "rep", 5, 1)
+    return whole.reshape(cores * chips * width)[:n]
 
 
 def shards(grad_blocks, gain_grads, first_moment, second_moment, master_flat, ema_flat):

time: 125 us -> 137 us (1.096); the launches traced: 124 us -> 135 us
  Pallas kernels: 90.1 us -> 96.2 us
  other arithmetic: 8.91 us -> 12.1 us
    pallas_call x4 -> x6, Pallas kernels: 90.1 us -> 96.2 us  [all_to_all(): pl.pallas_call(functools.partial(_a2a_kernel, axis, other_axis, stride, n...]
    reduce_sum x1 -> x2, other arithmetic: 1.05 us -> 2.72 us  [the longest x1 1.76 us: rep_sum(): half = jnp.sum(exchange(padded, 'rep', 0, 1), axis=0)]
    broadcast_in_dim x1 -> x2, local copies, waits for them, and re-layouts: 0.8 us -> 2.44 us  [the longest x1 1.74 us: rep_sum(): jnp.broadcast_to(every.reshape(1, chips * width), (cores, chips * width))]
    unnamed x22 -> x21, local copies, waits for them, and re-layouts: 9.79 us -> 8.72 us
where the time goes in v4:
time: 137 us; the launch traced here: 135 us
  Pallas kernels  96.2 us (70%)
  local copies, waits for them, and re-layouts  23.7 us (17%)
  other arithmetic  12.1 us (9%)
  between operations  2.98 us (2%)
    pallas_call x6, Pallas kernels, all_to_all(): pl.pallas_call(functools.partial(_a2a_kernel, axis, other_axis, stride, n...  96.2 us
    unnamed x21, local copies, waits for them, and re-layouts  8.72 us
    another operation x1, other arithmetic  4.98 us
    reshape x2, local copies, waits for them, and re-layouts, shards(): got2[:, :2 * piece].reshape(owners, 2, own_rows, cols).transpose(1, 0, 2, 3)  3.43 us

profile of v4, /device:TPU:6, one launch (start us, length us, event | category | flops | bytes accessed | tf_op | source)
XLA Modules:
  0.0 135.1 jit_solution(9156335929074097176)
XLA Ops:
  0.6 1.3 copy.19
  1.9 0.0 copy-start.7
  2.0 0.2 reshape_squeeze.3
  2.1 0.5 copy-done.7
  2.6 0.8 select_maximum_fusion
  3.4 8.8 %shard_map.109 = f32[2,448,128]{2,1,0:T(8,128)} custom-call(f32[2,448,128]{2,1,0:T(8,128)} %bitcast.38), custom_call_target="tpu_custom_call" | custom-call | tf_op jit(solution)/shard_map/pallas_call | solution.py:78
  12.2 1.8 %reduce_sum.45 = f32[448,128]{1,0:T(8,128)} reduce(f32[2,448,128]{2,1,0:T(8,128)} %shard_map.109, f32[]{:T(128)} %constant.16.clone.1), dimensions={0}, to_apply=%region_0.1 | reduce | flops 57344 | bytes 688132 | tf_op jit(solution)/shard_map/reduce_sum | solution.py:106
  14.0 19.2 %shard_map.110 = f32[8,56,128]{2,1,0:T(8,128)} custom-call(f32[8,56,128]{2,1,0:T(8,128)} %bitcast.41), custom_call_target="tpu_custom_call" | custom-call | tf_op jit(solution)/shard_map/pallas_call | solution.py:78
  33.2 1.0 reduce_sum.46
  34.2 0.7 broadcast_in_dim.35.x_ref
  34.9 12.7 %shard_map.111 = f32[8,56,128]{2,1,0:T(8,128)} custom-call(f32[8,56,128]{2,1,0:T(8,128)} %broadcast_in_dim.35.x_ref), custom_call_target="tpu_custom_call" | custom-call | tf_op jit(solution)/shard_map/pallas_call | solution.py:78
  47.6 1.7 %broadcast_in_dim.37.x_ref = f32[2,448,128]{2,1,0:T(8,128)} broadcast(f32[448,128]{1,0:T(8,128)} %bitcast.42), dimensions={1,2} | broadcast | bytes 688128 | tf_op jit(solution)/shard_map/broadcast_in_dim | solution.py:109
  49.3 8.8 %shard_map.112 = f32[2,448,128]{2,1,0:T(8,128)} custom-call(f32[2,448,128]{2,1,0:T(8,128)} %broadcast_in_dim.37.x_ref), custom_call_target="tpu_custom_call" | custom-call | tf_op jit(solution)/shard_map/pallas_call | solution.py:78
  58.1 1.3 fusion.6
  59.4 1.0 slice.49
  60.5 0.0 copy-start
  60.5 0.1 reshape_reshape.16
  60.5 0.9 copy-done
  61.5 0.2 slice.39
  61.7 0.8 fusion
  63.8 0.1 concatenate.29
  63.9 0.9 copy.24
  64.8 25.0 %shard_map.113 = f32[32,32,128]{2,1,0:T(8,128)} custom-call(f32[32,32,128]{2,1,0:T(8,128)} %bitcast.32), custom_call_target="tpu_custom_call" | custom-call | tf_op jit(solution)/shard_map/pallas_call | solution.py:78
  89.8 1.3 copy.31
  91.2 0.6 slice_reduce_fusion.1
  92.6 0.3 reshape.130
  92.8 0.0 copy-start.6
  92.9 0.2 copy.20
  93.0 0.0 copy-start.4
  93.0 0.0 copy-start.5
  93.1 0.5 concatenate.30
  93.6 0.3 copy-done.6
  93.9 0.2 copy-done.4
  94.1 0.1 copy-done.5
  94.2 5.0 %fusion.4 = (bf16[1,106896]{1,0:T(2,128)(2,1)S(1)}, f32[1,106896]{1,0:T(1,128)S(1)}, f32[1,106896]{1,0:T(1,128)}, f32[1,106896]{1,0:T(1,128)}) fusion(f32[1,106896]{1,0:T(1,128)S(1)} %copy-done.4, f32[]{:T(128)S(6)} %mul.87, f32[1,400]{1,0:T(1,128)S(1)} %bitcast.43, f32[1,106496]{1,0:T(1,128)S(1)} %concatenate.30, f32[1,106896]{1,0:T(1,128)S(1)} %copy-done.5, ...), kind=kLoop, calls=%fused_computation.21 | loop fusion | flops 2137920 | bytes 3206884 | tf_op jit(solution)/shard_map/convert.2
  99.2 0.0 copy-start.1
  99.2 1.2 slice_reduce_fusion
  100.4 0.2 stack.9
  100.6 0.0 copy-start.3
  100.6 0.2 copy.21
  100.8 0.0 copy-done.1
  100.8 0.8 copy-done.3
  101.7 0.7 multiply_add_fusion
  102.4 0.0 copy-start.2
  102.4 1.1 fusion.3
  103.5 0.2 stack.10
  103.7 0.0 copy-done.2
  103.7 0.2 copy.22
  103.9 0.2 maximum_bitcast_fusion
  104.1 0.6 reshape.131
  104.7 0.3 concatenate.33
  105.0 0.9 copy.26
  105.9 21.7 %shard_map.114 = bf16[32,64,128]{2,1,0:T(8,128)(2,1)} custom-call(bf16[32,64,128]{2,1,0:T(8,128)(2,1)} %bitcast.34), custom_call_target="tpu_custom_call" | custom-call | tf_op jit(solution)/shard_map/pallas_call | solution.py:78
  127.6 1.4 %copy.30 = bf16[4,8,64,128]{3,1,2,0:T(8,128)(2,1)S(1)} copy(bf16[4,8,64,128]{3,2,1,0:T(8,128)(2,1)} %bitcast.35) | data formatting | bytes 1048576
  129.0 0.7 reshape.136
  129.8 0.8 reshape.134
  130.5 1.8 %copy.23 = bf16[2,32,52,64]{2,1,3,0:T(8,128)(2,1)S(1)} copy(bf16[2,32,52,64]{3,2,0,1:T(8,128)(2,1)S(1)} %bitcast.29) | data formatting | bytes 851968 | tf_op jit(solution)/shard_map/transpose | solution.py:171
  132.4 2.7 %reshape.135 = bf16[2,1664,64]{1,2,0:T(8,128)(2,1)} reshape(bf16[2,32,52,64]{2,1,3,0:T(8,128)(2,1)S(1)} %copy.23) | data formatting | bytes 851968 | tf_op jit(solution)/shard_map/reshape | solution.py:171
  (8 shorter events, 0.1 us)
Async XLA Ops:
  1.9 0.7 copy-start.7
  60.5 1.0 copy-start
  92.8 1.0 copy-start.6
  93.0 1.0 copy-start.4
  93.0 1.2 copy-start.5
  99.2 1.6 %copy-start.1 = (f32[1,106896]{1,0:T(1,128)}, f32[1,106896]{1,0:T(1,128)S(1)}, u32[]{:S(2)}) copy-start(f32[1,106896]{1,0:T(1,128)S(1)} %get-tuple-element.7) | copy-start | bytes 1282756
  100.6 1.0 copy-start.3
  102.4 1.3 copy-start.2

commit v5 on v2

--- a/solution.py
+++ b/solution.py
@@ -35,23 +35,23 @@
     block = grad_blocks[0].reshape(owners, replicas, sub).transpose(1, 0, 2).reshape(replicas, owners * sub)
     gains_in = gain_grads[0].reshape(replicas, gsub)
     width = _pad_to(owners * sub + gsub)
-    send = jnp.concatenate(
-        [block, gains_in, jnp.zeros((replicas, width - owners * sub - gsub), jnp.float32)], axis=1
-    )
+    send = jnp.pad(jnp.concatenate([block, gains_in], axis=1), ((0, 0), (0, width - owners * sub - gsub)))
     got = lax.all_to_all(send, "rep", split_axis=0, concat_axis=0, tiled=True)
     mine = jnp.sum(got, axis=0)
     chunk = mine[: owners * sub].reshape(owners, sub)
     gain_chunk = mine[owners * sub : owners * sub + gsub]
     partial_value = jnp.sum(chunk * chunk) + jnp.sum(gain_chunk * gain_chunk)
     width2 = _pad_to(sub + gsub + 1)
-    rowdata = jnp.concatenate(
-        [
-            chunk,
-            jnp.broadcast_to(gain_chunk[None], (owners, gsub)),
-            jnp.broadcast_to(partial_value, (owners, 1)),
-            jnp.zeros((owners, width2 - sub - gsub - 1), jnp.float32),
-        ],
-        axis=1,
+    rowdata = jnp.pad(
+        jnp.concatenate(
+            [
+                chunk,
+                jnp.broadcast_to(gain_chunk[None], (owners, gsub)),
+                jnp.broadcast_to(partial_value, (owners, 1)),
+            ],
+            axis=1,
+        ),
+        ((0, 0), (0, width2 - sub - gsub - 1)),
     )
     send2 = jnp.broadcast_to(rowdata[None], (replicas, owners, width2)).reshape(replicas * owners, width2)
     got2 = lax.all_to_all(send2, ("rep", "shard"), split_axis=0, concat_axis=0, tiled=True)
@@ -63,10 +63,10 @@
     small_part = lax.dynamic_index_in_dim(got2[:, :, sub : sub + gsub], me, axis=1, keepdims=False)
     small_part = small_part.reshape(small)
     main_len = own_rows * owners * cols
-    grads = jnp.concatenate([owned.reshape(main_len), small_part]).reshape(1, -1) / replicas
+    grads = jnp.concatenate([owned.reshape(main_len), small_part]).reshape(1, -1)
     rms = jnp.sqrt(total / PARAMS)
     clip = jnp.minimum(1.0, 1.0 / (rms + clip_eps))
-    clipped = grads * clip
+    clipped = grads * (clip / replicas)
     new_first = beta_one * first_moment + (1.0 - beta_one) * clipped
     new_second = beta_two * second_moment + (1.0 - beta_two) * clipped * clipped
     update = (
@@ -84,13 +84,9 @@
     back = stacked.transpose(2, 0, 1, 3).reshape(owners, 2 * piece)
     gains_mine = new_master[0, main_len:].astype(jnp.bfloat16)
     width2 = _pad_to(2 * piece + small)
-    send2 = jnp.concatenate(
-        [
-            back,
-            jnp.broadcast_to(gains_mine[None], (owners, small)),
-            jnp.zeros((owners, width2 - 2 * piece - small), jnp.bfloat16),
-        ],
-        axis=1,
+    send2 = jnp.pad(
+        jnp.concatenate([back, jnp.broadcast_to(gains_mine[None], (owners, small))], axis=1),
+        ((0, 0), (0, width2 - 2 * piece - small)),
     )
     got2 = lax.all_to_all(send2, "shard", split_axis=0, concat_axis=0, tiled=True)
     weight_blocks = (

time: 119 us -> 118 us (level)
  blocking collectives: 20 us -> 43.5 us
  waiting for transfers between devices: 34.3 us -> 20.7 us
  starting transfers between devices: 28.6 us -> 18.5 us
    all_to_all x0 -> x1, blocking collectives: none -> 23.5 us  [shards(): got = lax.all_to_all(send, 'rep', split_axis=0, concat_axis=0, tiled=True)]
    all_to_all x1 -> x0, waiting for transfers between devices: 13.6 us -> none  [shards(): got = lax.all_to_all(send, 'rep', split_axis=0, concat_axis=0, tiled=True)]
    all_to_all x1 -> x0, starting transfers between devices: 10.1 us -> none  [shards(): got = lax.all_to_all(send, 'rep', split_axis=0, concat_axis=0, tiled=True)]
  transfers between devices with their start and end apart: 2 -> 1, of which waited for: 2 -> 1; matrix products, arithmetic and copies ran while one was open for 0% -> 0% of each run, Pallas kernels for 0% -> 0%
where the time goes in v5:
time: 118 us; the launch traced here: 116 us
  blocking collectives  43.5 us (37%)
  waiting for transfers between devices  20.7 us (18%)
  local copies, waits for them, and re-layouts  19.5 us (17%)
  starting transfers between devices  18.5 us (16%)
  other arithmetic  10.5 us (9%)
  between operations  3 us (3%)
    all_to_all x1, blocking collectives, shards(): got = lax.all_to_all(send, 'rep', split_axis=0, concat_axis=0, tiled=True)  23.5 us
    all_to_all x1, waiting for transfers between devices, shards(): lax.all_to_all(send2, ('rep', 'shard'), split_axis=0, concat_axis=0, tile...  20.7 us
    all_to_all x1, blocking collectives, shards(): lax.all_to_all(send2, 'shard', split_axis=0, concat_axis=0, tiled=True)  20 us
    all_to_all x1, starting transfers between devices, shards(): lax.all_to_all(send2, ('rep', 'shard'), split_axis=0, concat_axis=0, tile...  18.5 us
    another operation x1, other arithmetic  4.98 us
    unnamed x18, local copies, waits for them, and re-layouts  4.15 us
    reshape x2, local copies, waits for them, and re-layouts, shards(): got2[:, :2 * piece].reshape(owners, 2, own_rows, cols).transpose(1, 0, 2, 3)  3.43 us
  transfers between devices with their start and end apart: 1, of which 1 were waited for; matrix products, arithmetic and copies ran while one was open for 0% of the time, Pallas kernels for 0%

profile of v5, /device:TPU:6, one launch (start us, length us, event | category | flops | bytes accessed | tf_op | source)
XLA Modules:
  0.0 115.7 jit_solution(16902203978617292275)
XLA Ops:
  0.6 0.5 broadcast.85
  1.1 1.3 %reduce.16 = f32[400]{0:T(512)S(1)} reduce(f32[1,400]{1,0:T(1,128)} %param.7, f32[]{:T(128)} %broadcast.85), dimensions={0}, to_apply=%param.7.reduce_sub_computation.3 | reduce | bytes 3204 | tf_op args[1]
  2.5 0.1 reshape_squeeze.7
  2.6 1.3 %copy.35 = f32[1,1664,64]{2,1,0:T(8,128)S(1)} copy(f32[1,1664,64]{1,2,0:T(8,128)} %param.6) | data formatting | bytes 851968 | tf_op args[0]
  3.9 0.4 reshape_squeeze.6
  4.3 0.3 copy.36
  4.6 0.3 reshape.122
  4.9 0.4 copy.37
  5.4 23.5 %all_to_all.30 = f32[16,1,6784]{2,1,0:T(1,128)S(1)} all-to-all(f32[16,1,6784]{2,1,0:T(1,128)S(1)} %copy.37), channel_id=1, replica_groups=mesh['rep'=16,'shard'=32] {'rep'}, dimensions={0} | all-to-all | bytes 868352 | tf_op jit(solution)/shard_map/all_to_all | solution.py:39
  28.9 0.3 reduce_sum.36
  29.2 0.6 fusion.6
  29.8 0.6 multiply_reduce_fusion
  30.4 0.1 pad.22.clone
  31.8 0.1 pad.23.clone
  31.8 0.1 reshape.123
  32.0 1.3 %all_to_all.22 = f32[512,1,256]{2,1,0:T(1,128)} reshape(f32[16,32,256]{2,1,0:T(8,128)S(1)} %broadcast_in_dim.30) | data formatting | bytes 1048576 | tf_op jit(solution)/shard_map/all_to_all | solution.py:57
  33.3 18.5 %all-to-all-start.1 = ((f32[512,1,256]{2,1,0:T(1,128)}), f32[512,1,256]{2,1,0:T(1,128)S(1)}, u32[]{:S(2)}, u32[]{:S(2)}) async-start(f32[512,1,256]{2,1,0:T(1,128)} %all_to_all.22), calls=%async_computation.1 | async-start | bytes 1048576 | tf_op jit(solution)/shard_map/all_to_all | solution.py:57
  51.9 20.7 %all-to-all-done.1 = f32[512,1,256]{2,1,0:T(1,128)S(1)} async-done(((f32[512,1,256]{2,1,0:T(1,128)}), f32[512,1,256]{2,1,0:T(1,128)S(1)}, u32[]{:S(2)}, u32[]{:S(2)}) %all-to-all-start.1) | async-done | bytes 524320 | tf_op jit(solution)/shard_map/all_to_all | solution.py:57
  72.6 0.7 slice_reduce_fusion.1
  73.4 0.1 slice.46
  74.3 0.1 concatenate.31
  74.4 0.3 copy.38
  74.7 0.6 reshape.125
  75.4 0.0 copy-start.5
  75.4 0.2 copy.39
  75.6 0.0 copy-start.3
  75.6 0.0 copy-start.4
  75.6 0.5 concatenate.30
  76.1 0.3 copy-done.5
  76.4 0.2 copy-done.3
  76.6 0.1 copy-done.4
  76.8 5.0 %fusion.4 = (bf16[1,106896]{1,0:T(2,128)(2,1)S(1)}, f32[1,106896]{1,0:T(1,128)S(1)}, f32[1,106896]{1,0:T(1,128)}, f32[1,106896]{1,0:T(1,128)}) fusion(f32[1,106896]{1,0:T(1,128)S(1)} %copy-done.3, f32[]{:T(128)S(6)} %div.27, f32[1,400]{1,0:T(1,128)S(1)} %concatenate.31, f32[1,106496]{1,0:T(1,128)S(1)} %concatenate.30, f32[1,106896]{1,0:T(1,128)S(1)} %copy-done.4, ...), kind=kLoop, calls=%fused_computation.25 | loop fusion | flops 2137920 | bytes 3206884 | tf_op jit(solution)/shard_map/convert.2
  81.7 0.0 copy-start
  81.8 1.2 %slice_reduce_fusion = bf16[106496]{0:T(1024)(128)(2,1)S(1)} fusion(bf16[1,106896]{1,0:T(2,128)(2,1)S(1)} %get-tuple-element.6), kind=kLoop, calls=%fused_computation.18 | loop fusion | bytes 425984 | tf_op jit(solution)/shard_map/slice | solution.py:81
  83.0 0.2 stack.9
  83.2 0.0 copy-start.2
  83.2 0.2 copy.40
  83.4 0.0 copy-done
  83.4 0.8 copy-done.2
  84.2 0.7 multiply_add_fusion
  84.9 0.0 copy-start.1
  84.9 1.1 fusion.3
  86.1 0.2 stack.10
  86.3 0.0 copy-done.1
  86.3 0.2 copy.41
  86.5 0.2 maximum_bitcast_fusion
  86.7 0.6 reshape.126
  87.3 0.1 pad_maximum_fusion
  87.4 0.5 broadcast.90
  87.9 0.9 reduce.17
  88.8 0.3 reshape.150
  89.2 20.0 %all_to_all.31 = bf16[32,2,3584]{2,1,0:T(2,128)(2,1)S(1)} all-to-all(bf16[32,2,3584]{2,1,0:T(2,128)(2,1)S(1)} %reshape.150), channel_id=1, replica_groups=mesh['rep'=16,'shard'=32] {'shard'}, dimensions={0} | all-to-all | bytes 917504 | tf_op jit(solution)/shard_map/all_to_all | solution.py:91
  109.1 0.4 reshape.151
  109.5 0.2 copy.47
  109.7 0.7 reshape.129
  110.4 0.8 reshape.127
  111.2 1.8 %copy.43 = bf16[2,32,52,64]{2,1,3,0:T(8,128)(2,1)S(1)} copy(bf16[2,32,52,64]{3,2,0,1:T(8,128)(2,1)S(1)} %bitcast.24) | data formatting | bytes 851968 | tf_op jit(solution)/shard_map/transpose | solution.py:93
  113.1 2.7 %reshape.128 = bf16[2,1664,64]{1,2,0:T(8,128)(2,1)} reshape(bf16[2,32,52,64]{2,1,3,0:T(8,128)(2,1)S(1)} %copy.43) | data formatting | bytes 851968 | tf_op jit(solution)/shard_map/reshape | solution.py:93
  (12 shorter events, 0.3 us)
Async XLA Ops:
  33.3 39.3 %all-to-all-start.1 = ((f32[512,1,256]{2,1,0:T(1,128)}), f32[512,1,256]{2,1,0:T(1,128)S(1)}, u32[]{:S(2)}, u32[]{:S(2)}) async-start(f32[512,1,256]{2,1,0:T(1,128)} %all_to_all.22), calls=%async_computation.1 | async-start | bytes 1048576 | tf_op jit(solution)/shard_map/all_to_all | solution.py:57
  75.4 1.0 copy-start.5
  75.6 1.0 copy-start.3
  75.6 1.2 %copy-start.4 = (f32[1,106896]{1,0:T(1,128)S(1)}, f32[1,106896]{1,0:T(1,128)}, u32[]{:S(2)}) copy-start(f32[1,106896]{1,0:T(1,128)} %param.9) | copy-start | bytes 1282756
  81.7 1.6 %copy-start = (f32[1,106896]{1,0:T(1,128)}, f32[1,106896]{1,0:T(1,128)S(1)}, u32[]{:S(2)}) copy-start(f32[1,106896]{1,0:T(1,128)S(1)} %get-tuple-element.7) | copy-start | bytes 1282756
  83.2 1.0 copy-start.2
  84.9 1.3 %copy-start.1 = (f32[1,106896]{1,0:T(1,128)}, f32[1,106896]{1,0:T(1,128)S(1)}, u32[]{:S(2)}) copy-start(f32[1,106896]{1,0:T(1,128)S(1)} %multiply_add_fusion) | copy-start | bytes 1282756

commit v6 on v5

--- a/solution.py
+++ b/solution.py
@@ -1,7 +1,13 @@
 import jax
 import jax.numpy as jnp
 from jax import lax
+import functools
+
+from jax.experimental import pallas as pl
+from jax.experimental.pallas import tpu as pltpu
 from jax.sharding import PartitionSpec as P
+
+MESH = pl.DeviceIdType.MESH
 
 STEP = 100
 PARAMS = 3420672
@@ -22,6 +28,64 @@
     return -(-n // LANE) * LANE
 
 
+def _rs_kernel(n, main_rows, tail, x_ref, o_ref, p_ref, recv, send_sem, recv_sem, local_sem):
+    me = lax.axis_index("rep")
+    shard = lax.axis_index("shard")
+    barrier = pltpu.get_barrier_semaphore()
+    for k in range(1, n):
+        pl.semaphore_signal(barrier, inc=1, device_id=(lax.rem(me + k, n), shard), device_id_type=MESH)
+    pl.semaphore_wait(barrier, n - 1)
+    local = pltpu.make_async_copy(x_ref.at[me], recv.at[me], local_sem)
+    local.start()
+
+    def copy(k, j, src):
+        return pltpu.make_async_remote_copy(
+            src_ref=x_ref.at[j],
+            dst_ref=recv.at[src],
+            send_sem=send_sem.at[k],
+            recv_sem=recv_sem.at[k],
+            device_id=(j, shard),
+            device_id_type=MESH,
+        )
+
+    for k in range(1, n):
+        copy(k, lax.rem(me + k, n), me).start()
+    local.wait()
+    for k in range(1, n):
+        c = copy(k, lax.rem(me + k, n), lax.rem(me + n - k, n))
+        c.wait_send()
+        c.wait_recv()
+    total = recv[0]
+    for k in range(1, n):
+        total = total + recv[k]
+    o_ref[...] = total
+    row = lax.broadcasted_iota(jnp.int32, total.shape, 0)
+    lane = lax.broadcasted_iota(jnp.int32, total.shape, 1)
+    keep = (row < main_rows) | ((row == main_rows) & (lane < tail))
+    squares = jnp.where(keep, total * total, 0.0)
+    p_ref[...] = jnp.broadcast_to(jnp.sum(squares), p_ref.shape)
+
+
+def reduce_scatter(x, used, collective_id):
+    n, rows, lanes = x.shape
+    return pl.pallas_call(
+        functools.partial(_rs_kernel, n, used // lanes, used % lanes),
+        out_shape=(
+            jax.ShapeDtypeStruct((rows, lanes), x.dtype),
+            jax.ShapeDtypeStruct((8, lanes), x.dtype),
+        ),
+        in_specs=[pl.BlockSpec(memory_space=pl.ANY)],
+        out_specs=(pl.BlockSpec(memory_space=pltpu.VMEM), pl.BlockSpec(memory_space=pltpu.VMEM)),
+        scratch_shapes=[
+            pltpu.VMEM((n, rows, lanes), x.dtype),
+            pltpu.SemaphoreType.DMA((n,)),
+            pltpu.SemaphoreType.DMA((n,)),
+            pltpu.SemaphoreType.DMA,
+        ],
+        compiler_params=pltpu.CompilerParams(collective_id=collective_id, has_side_effects=True),
+    )(x)
+
+
 def shards(grad_blocks, gain_grads, first_moment, second_moment, master_flat, ema_flat):
     replicas = lax.axis_size("rep")
     owners = lax.axis_size("shard")
@@ -34,13 +98,13 @@
     gsub = small // replicas
     block = grad_blocks[0].reshape(owners, replicas, sub).transpose(1, 0, 2).reshape(replicas, owners * sub)
     gains_in = gain_grads[0].reshape(replicas, gsub)
-    width = _pad_to(owners * sub + gsub)
+    width = -(-(owners * sub + gsub) // (8 * LANE)) * 8 * LANE
     send = jnp.pad(jnp.concatenate([block, gains_in], axis=1), ((0, 0), (0, width - owners * sub - gsub)))
-    got = lax.all_to_all(send, "rep", split_axis=0, concat_axis=0, tiled=True)
-    mine = jnp.sum(got, axis=0)
+    mine, partial = reduce_scatter(send.reshape(replicas, width // LANE, LANE), owners * sub + gsub, 0)
+    mine = mine.reshape(width)
     chunk = mine[: owners * sub].reshape(owners, sub)
     gain_chunk = mine[owners * sub : owners * sub + gsub]
-    partial_value = jnp.sum(chunk * chunk) + jnp.sum(gain_chunk * gain_chunk)
+    partial_value = partial[0, 0]
     width2 = _pad_to(sub + gsub + 1)
     rowdata = jnp.pad(
         jnp.concatenate(

time: 118 us -> 118 us (level)
  Pallas kernels: 0 us -> 24.7 us
  blocking collectives: 43.5 us -> 20 us
  local copies, waits for them, and re-layouts: 19.5 us -> 23.1 us
  starting transfers between devices: 18.5 us -> 16 us
  other arithmetic: 10.5 us -> 9.04 us
  between operations: 3 us -> 1.7 us
    pallas_call x0 -> x1, Pallas kernels: none -> 24.7 us  [reduce_scatter(): pl.pallas_call(functools.partial(_rs_kernel, n, used // lanes, used % lan...]
    all_to_all x1 -> x0, blocking collectives: 23.5 us -> none  [shards(): got = lax.all_to_all(send, 'rep', split_axis=0, concat_axis=0, tiled=True)]
    all_to_all x1, starting transfers between devices: 18.5 us -> 16 us  [shards(): lax.all_to_all(send2, ('rep', 'shard'), split_axis=0, concat_axis=0, tile...]
    slice x0 -> x2, local copies, waits for them, and re-layouts: none -> 1.88 us  [the longest x1 1.19 us: shards(): partial_value = partial[0, 0]]
    unnamed x18 -> x19, local copies, waits for them, and re-layouts: 4.15 us -> 5.01 us
where the time goes in v6:
time: 118 us; the launch traced here: 115 us
  Pallas kernels  24.7 us (21%)
  local copies, waits for them, and re-layouts  23.1 us (20%)
  waiting for transfers between devices  20.7 us (18%)
  blocking collectives  20 us (17%)
  starting transfers between devices  16 us (14%)
  other arithmetic  9.04 us (8%)
  between operations  1.7 us (1%)
    pallas_call x1, Pallas kernels, reduce_scatter(): pl.pallas_call(functools.partial(_rs_kernel, n, used // lanes, used % lan...  24.7 us
    all_to_all x1, waiting for transfers between devices, shards(): lax.all_to_all(send2, ('rep', 'shard'), split_axis=0, concat_axis=0, tile...  20.7 us
    all_to_all x1, blocking collectives, shards(): lax.all_to_all(send2, 'shard', split_axis=0, concat_axis=0, tiled=True)  20 us
    all_to_all x1, starting transfers between devices, shards(): lax.all_to_all(send2, ('rep', 'shard'), split_axis=0, concat_axis=0, tile...  16 us
    unnamed x19, local copies, waits for them, and re-layouts  5.01 us
    another operation x1, other arithmetic  4.98 us
    reshape x2, local copies, waits for them, and re-layouts, shards(): got2[:, :2 * piece].reshape(owners, 2, own_rows, cols).transpose(1, 0, 2, 3)  3.43 us
  transfers between devices with their start and end apart: 1, of which 1 were waited for; matrix products, arithmetic and copies ran while one was open for 0% of the time, Pallas kernels for 0%

profile of v6, /device:TPU:6, one launch (start us, length us, event | category | flops | bytes accessed | tf_op | source)
XLA Modules:
  0.0 115.4 jit_solution(4347606516948684661)
XLA Ops:
  0.6 0.5 broadcast.85
  1.1 1.3 %reduce.14 = f32[400]{0:T(512)S(1)} reduce(f32[1,400]{1,0:T(1,128)} %param.7, f32[]{:T(128)} %broadcast.85), dimensions={0}, to_apply=%param.7.reduce_sub_computation.3 | reduce | bytes 3204 | tf_op args[1]
  2.5 0.1 reshape_squeeze.7
  2.6 1.3 %copy.33 = f32[1,1664,64]{2,1,0:T(8,128)S(1)} copy(f32[1,1664,64]{1,2,0:T(8,128)} %param.6) | data formatting | bytes 851968 | tf_op args[0]
  3.9 0.4 reshape_squeeze.6
  4.3 0.3 copy.34
  4.6 0.3 reshape.128
  4.9 0.9 copy.43
  5.8 24.7 %shard_map.109 = (f32[56,128]{1,0:T(8,128)}, f32[8,128]{1,0:T(8,128)}) custom-call(f32[16,56,128]{2,1,0:T(8,128)} %bitcast.31), custom_call_target="tpu_custom_call" | custom-call | tf_op jit(solution)/shard_map/pallas_call | solution.py:71
  30.5 1.2 %slice.39 = f32[1,1]{1,0:T(1,128)} slice(f32[8,128]{1,0:T(8,128)} %get-tuple-element.9), slice={[0:1], [0:1]} | slice | bytes 8 | tf_op jit(solution)/shard_map/slice | solution.py:107
  31.7 0.7 slice.48
  32.4 0.1 pad.22.clone
  32.5 0.7 pad.23.clone
  33.2 0.8 reshape.130
  34.1 1.3 %all_to_all.14 = f32[512,1,256]{2,1,0:T(1,128)} reshape(f32[16,32,256]{2,1,0:T(8,128)S(1)} %broadcast_in_dim.30) | data formatting | bytes 1048576 | tf_op jit(solution)/shard_map/all_to_all | solution.py:121
  35.5 16.0 %all-to-all-start = ((f32[512,1,256]{2,1,0:T(1,128)}), f32[512,1,256]{2,1,0:T(1,128)S(1)}, u32[]{:S(2)}, u32[]{:S(2)}) async-start(f32[512,1,256]{2,1,0:T(1,128)} %all_to_all.14), calls=%async_computation | async-start | bytes 1048576 | tf_op jit(solution)/shard_map/all_to_all | solution.py:121
  51.5 20.7 %all-to-all-done = f32[512,1,256]{2,1,0:T(1,128)S(1)} async-done(((f32[512,1,256]{2,1,0:T(1,128)}), f32[512,1,256]{2,1,0:T(1,128)S(1)}, u32[]{:S(2)}, u32[]{:S(2)}) %all-to-all-start) | async-done | bytes 524320 | tf_op jit(solution)/shard_map/all_to_all | solution.py:121
  72.3 0.7 slice_reduce_fusion.1
  73.0 0.1 slice.50
  74.0 0.1 concatenate.31
  74.0 0.3 copy.35
  74.4 0.6 reshape.133
  75.0 0.0 copy-start.5
  75.0 0.2 copy.36
  75.2 0.0 copy-start.3
  75.2 0.0 copy-start.4
  75.2 0.5 concatenate.30
  75.8 0.3 copy-done.5
  76.0 0.2 copy-done.3
  76.2 0.1 copy-done.4
  76.4 5.0 %fusion.4 = (bf16[1,106896]{1,0:T(2,128)(2,1)S(1)}, f32[1,106896]{1,0:T(1,128)S(1)}, f32[1,106896]{1,0:T(1,128)}, f32[1,106896]{1,0:T(1,128)}) fusion(f32[1,106896]{1,0:T(1,128)S(1)} %copy-done.3, f32[]{:T(128)S(6)} %div.27, f32[1,400]{1,0:T(1,128)S(1)} %concatenate.31, f32[1,106496]{1,0:T(1,128)S(1)} %concatenate.30, f32[1,106896]{1,0:T(1,128)S(1)} %copy-done.4, ...), kind=kLoop, calls=%fused_computation.23 | loop fusion | flops 2137920 | bytes 3206884 | tf_op jit(solution)/shard_map/convert.2
  81.4 0.0 copy-start
  81.4 1.2 %slice_reduce_fusion = bf16[106496]{0:T(1024)(128)(2,1)S(1)} fusion(bf16[1,106896]{1,0:T(2,128)(2,1)S(1)} %get-tuple-element.10), kind=kLoop, calls=%fused_computation.18 | loop fusion | bytes 425984 | tf_op jit(solution)/shard_map/slice | solution.py:145
  82.6 0.2 stack.9
  82.8 0.0 copy-start.2
  82.8 0.2 copy.37
  83.0 0.0 copy-done
  83.0 0.8 copy-done.2
  83.8 0.7 multiply_add_fusion
  84.6 0.0 copy-start.1
  84.6 1.1 fusion.3
  85.7 0.2 stack.10
  85.9 0.0 copy-done.1
  85.9 0.2 copy.38
  86.1 0.2 maximum_bitcast_fusion
  86.3 0.6 reshape.134
  86.9 0.1 pad_maximum_fusion
  87.0 0.5 broadcast.90
  87.5 0.9 reduce.15
  88.5 0.3 reshape.158
  88.8 20.0 %all_to_all.21 = bf16[32,2,3584]{2,1,0:T(2,128)(2,1)S(1)} all-to-all(bf16[32,2,3584]{2,1,0:T(2,128)(2,1)S(1)} %reshape.158), channel_id=1, replica_groups=mesh['rep'=16,'shard'=32] {'shard'}, dimensions={0} | all-to-all | bytes 917504 | tf_op jit(solution)/shard_map/all_to_all | solution.py:155
  108.8 0.4 reshape.159
  109.1 0.2 copy.45
  109.3 0.7 reshape.137
  110.1 0.8 reshape.135
  110.8 1.8 %copy.40 = bf16[2,32,52,64]{2,1,3,0:T(8,128)(2,1)S(1)} copy(bf16[2,32,52,64]{3,2,0,1:T(8,128)(2,1)S(1)} %bitcast.29) | data formatting | bytes 851968 | tf_op jit(solution)/shard_map/transpose | solution.py:157
  112.7 2.7 %reshape.136 = bf16[2,1664,64]{1,2,0:T(8,128)(2,1)} reshape(bf16[2,32,52,64]{2,1,3,0:T(8,128)(2,1)S(1)} %copy.40) | data formatting | bytes 851968 | tf_op jit(solution)/shard_map/reshape | solution.py:157
  (12 shorter events, 0.3 us)
Async XLA Ops:
  35.5 36.8 %all-to-all-start = ((f32[512,1,256]{2,1,0:T(1,128)}), f32[512,1,256]{2,1,0:T(1,128)S(1)}, u32[]{:S(2)}, u32[]{:S(2)}) async-start(f32[512,1,256]{2,1,0:T(1,128)} %all_to_all.14), calls=%async_computation | async-start | bytes 1048576 | tf_op jit(solution)/shard_map/all_to_all | solution.py:121
  75.0 1.0 copy-start.5
  75.2 1.0 copy-start.3
  75.2 1.2 %copy-start.4 = (f32[1,106896]{1,0:T(1,128)S(1)}, f32[1,106896]{1,0:T(1,128)}, u32[]{:S(2)}) copy-start(f32[1,106896]{1,0:T(1,128)} %param.9) | copy-start | bytes 1282756
  81.4 1.6 %copy-start = (f32[1,106896]{1,0:T(1,128)}, f32[1,106896]{1,0:T(1,128)S(1)}, u32[]{:S(2)}) copy-start(f32[1,106896]{1,0:T(1,128)S(1)} %get-tuple-element.11) | copy-start | bytes 1282756
  82.8 1.0 copy-start.2
  84.6 1.3 %copy-start.1 = (f32[1,106896]{1,0:T(1,128)}, f32[1,106896]{1,0:T(1,128)S(1)}, u32[]{:S(2)}) copy-start(f32[1,106896]{1,0:T(1,128)S(1)} %multiply_add_fusion) | copy-start | bytes 1282756

commit v7 on v6

--- a/solution.py
+++ b/solution.py
@@ -28,7 +28,7 @@
     return -(-n // LANE) * LANE
 
 
-def _rs_kernel(n, main_rows, tail, x_ref, o_ref, p_ref, recv, send_sem, recv_sem, local_sem):
+def _rs_kernel(n, main, share, x_ref, o_ref, p_ref, recv, send_sem, recv_sem, local_sem):
     me = lax.axis_index("rep")
     shard = lax.axis_index("shard")
     barrier = pltpu.get_barrier_semaphore()
@@ -59,17 +59,20 @@
     for k in range(1, n):
         total = total + recv[k]
     o_ref[...] = total
-    row = lax.broadcasted_iota(jnp.int32, total.shape, 0)
-    lane = lax.broadcasted_iota(jnp.int32, total.shape, 1)
-    keep = (row < main_rows) | ((row == main_rows) & (lane < tail))
+    flat = (
+        lax.broadcasted_iota(jnp.int32, total.shape, 0) * total.shape[1]
+        + lax.broadcasted_iota(jnp.int32, total.shape, 1)
+    )
+    start = main + me * share
+    keep = (flat < main) | ((flat >= start) & (flat < start + share))
     squares = jnp.where(keep, total * total, 0.0)
     p_ref[...] = jnp.broadcast_to(jnp.sum(squares), p_ref.shape)
 
 
-def reduce_scatter(x, used, collective_id):
+def reduce_scatter(x, main, share, collective_id):
     n, rows, lanes = x.shape
     return pl.pallas_call(
-        functools.partial(_rs_kernel, n, used // lanes, used % lanes),
+        functools.partial(_rs_kernel, n, main, share),
         out_shape=(
             jax.ShapeDtypeStruct((rows, lanes), x.dtype),
             jax.ShapeDtypeStruct((8, lanes), x.dtype),
@@ -97,35 +100,26 @@
     sub = piece // replicas
     gsub = small // replicas
     block = grad_blocks[0].reshape(owners, replicas, sub).transpose(1, 0, 2).reshape(replicas, owners * sub)
-    gains_in = gain_grads[0].reshape(replicas, gsub)
-    width = -(-(owners * sub + gsub) // (8 * LANE)) * 8 * LANE
-    send = jnp.pad(jnp.concatenate([block, gains_in], axis=1), ((0, 0), (0, width - owners * sub - gsub)))
-    mine, partial = reduce_scatter(send.reshape(replicas, width // LANE, LANE), owners * sub + gsub, 0)
+    gains_in = jnp.broadcast_to(gain_grads, (replicas, small))
+    width = -(-(owners * sub + small) // (8 * LANE)) * 8 * LANE
+    send = jnp.pad(jnp.concatenate([block, gains_in], axis=1), ((0, 0), (0, width - owners * sub - small)))
+    mine, partial = reduce_scatter(send.reshape(replicas, width // LANE, LANE), owners * sub, gsub, 0)
     mine = mine.reshape(width)
     chunk = mine[: owners * sub].reshape(owners, sub)
-    gain_chunk = mine[owners * sub : owners * sub + gsub]
+    small_part = mine[owners * sub : owners * sub + small]
     partial_value = partial[0, 0]
-    width2 = _pad_to(sub + gsub + 1)
+    width2 = _pad_to(sub + 1)
     rowdata = jnp.pad(
-        jnp.concatenate(
-            [
-                chunk,
-                jnp.broadcast_to(gain_chunk[None], (owners, gsub)),
-                jnp.broadcast_to(partial_value, (owners, 1)),
-            ],
-            axis=1,
-        ),
-        ((0, 0), (0, width2 - sub - gsub - 1)),
+        jnp.concatenate([chunk, jnp.broadcast_to(partial_value, (owners, 1))], axis=1),
+        ((0, 0), (0, width2 - sub - 1)),
     )
     send2 = jnp.broadcast_to(rowdata[None], (replicas, owners, width2)).reshape(replicas * owners, width2)
     got2 = lax.all_to_all(send2, ("rep", "shard"), split_axis=0, concat_axis=0, tiled=True)
     got2 = got2.reshape(replicas, owners, width2)
-    total = jnp.sum(got2[:, :, sub + gsub]) / (replicas * replicas)
+    total = jnp.sum(got2[:, :, sub]) / (replicas * replicas)
     owned = (
         got2[:, :, :sub].transpose(1, 0, 2).reshape(owners, own_rows, cols).transpose(1, 0, 2)
     )
-    small_part = lax.dynamic_index_in_dim(got2[:, :, sub : sub + gsub], me, axis=1, keepdims=False)
-    small_part = small_part.reshape(small)
     main_len = own_rows * owners * cols
     grads = jnp.concatenate([owned.reshape(main_len), small_part]).reshape(1, -1)
     rms = jnp.sqrt(total / PARAMS)

time: 118 us -> 115 us (0.975)
  local copies, waits for them, and re-layouts: 23.1 us -> 21.9 us
    unnamed x2 -> x0, other arithmetic: 1.38 us -> none
    unnamed x19 -> x21, local copies, waits for them, and re-layouts: 5.01 us -> 4.91 us
  transfers between devices with their start and end apart: 1 -> 1, of which waited for: 1 -> 1; matrix products, arithmetic and copies ran while one was open for 0% -> 1% of each run, Pallas kernels for 0% -> 0%
where the time goes in v7:
time: 115 us; the launch traced here: 113 us
  Pallas kernels  24.7 us (21%)
  local copies, waits for them, and re-layouts  21.9 us (19%)
  waiting for transfers between devices  20.1 us (17%)
  blocking collectives  20 us (17%)
  starting transfers between devices  16 us (14%)
  other arithmetic  8.35 us (7%)
  between operations  1.67 us (1%)
    pallas_call x1, Pallas kernels, reduce_scatter(): pl.pallas_call(functools.partial(_rs_kernel, n, main, share), out_shape=(...  24.7 us
    all_to_all x1, waiting for transfers between devices, shards(): lax.all_to_all(send2, ('rep', 'shard'), split_axis=0, concat_axis=0, tile...  20.1 us
    all_to_all x1, blocking collectives, shards(): lax.all_to_all(send2, 'shard', split_axis=0, concat_axis=0, tiled=True)  20 us
    all_to_all x1, starting transfers between devices, shards(): lax.all_to_all(send2, ('rep', 'shard'), split_axis=0, concat_axis=0, tile...  16 us
    another operation x1, other arithmetic  4.98 us
    unnamed x21, local copies, waits for them, and re-layouts  4.91 us
    reshape x2, local copies, waits for them, and re-layouts, shards(): got2[:, :2 * piece].reshape(owners, 2, own_rows, cols).transpose(1, 0, 2, 3)  3.43 us
  transfers between devices with their start and end apart: 1, of which 1 were waited for; matrix products, arithmetic and copies ran while one was open for 1% of the time, Pallas kernels for 0%

profile of v7, /device:TPU:6, one launch (start us, length us, event | category | flops | bytes accessed | tf_op | source)
XLA Modules:
  0.0 112.7 jit_solution(1437003412551798822)
XLA Ops:
  0.6 1.3 %copy.31 = f32[1,1664,64]{2,1,0:T(8,128)S(1)} copy(f32[1,1664,64]{1,2,0:T(8,128)} %param.6) | data formatting | bytes 851968 | tf_op args[0]
  1.9 0.4 reshape_squeeze.3
  2.3 0.3 copy.32
  2.7 0.0 copy-start.6
  2.7 0.3 reshape.120
  3.0 0.4 copy-done.6
  3.4 0.9 copy.41
  4.3 24.7 %shard_map.109 = (f32[56,128]{1,0:T(8,128)}, f32[8,128]{1,0:T(8,128)}) custom-call(f32[16,56,128]{2,1,0:T(8,128)} %bitcast.30), custom_call_target="tpu_custom_call" | custom-call | tf_op jit(solution)/shard_map/pallas_call | solution.py:74
  29.0 1.2 %slice.35 = f32[1,1]{1,0:T(1,128)} slice(f32[8,128]{1,0:T(8,128)} %get-tuple-element.9), slice={[0:1], [0:1]} | slice | bytes 8 | tf_op jit(solution)/shard_map/slice | solution.py:110
  30.2 0.8 reshape.122
  31.1 0.7 pad_select_fusion
  31.8 1.3 %all_to_all.14 = f32[512,1,256]{2,1,0:T(1,128)} reshape(f32[16,32,256]{2,1,0:T(8,128)S(1)} %broadcast_in_dim.29) | data formatting | bytes 1048576 | tf_op jit(solution)/shard_map/all_to_all | solution.py:117
  33.1 16.0 %all-to-all-start = ((f32[512,1,256]{2,1,0:T(1,128)}), f32[512,1,256]{2,1,0:T(1,128)S(1)}, u32[]{:S(2)}, u32[]{:S(2)}) async-start(f32[512,1,256]{2,1,0:T(1,128)} %all_to_all.14), calls=%async_computation | async-start | bytes 1048576 | tf_op jit(solution)/shard_map/all_to_all | solution.py:117
  49.1 0.7 slice.45
  49.8 20.1 %all-to-all-done = f32[512,1,256]{2,1,0:T(1,128)S(1)} async-done(((f32[512,1,256]{2,1,0:T(1,128)}), f32[512,1,256]{2,1,0:T(1,128)S(1)}, u32[]{:S(2)}, u32[]{:S(2)}) %all-to-all-start) | async-done | bytes 524320 | tf_op jit(solution)/shard_map/all_to_all | solution.py:117
  69.9 0.7 slice_reduce_fusion.1
  71.4 0.3 copy.33
  71.7 0.6 reshape.124
  72.4 0.0 copy-start.5
  72.4 0.2 copy.34
  72.6 0.0 copy-start.3
  72.6 0.0 copy-start.4
  72.6 0.5 concatenate.30
  73.1 0.3 copy-done.5
  73.4 0.2 copy-done.3
  73.6 0.1 copy-done.4
  73.7 5.0 %fusion.3 = (bf16[1,106896]{1,0:T(2,128)(2,1)S(1)}, f32[1,106896]{1,0:T(1,128)S(1)}, f32[1,106896]{1,0:T(1,128)}, f32[1,106896]{1,0:T(1,128)}) fusion(f32[1,106896]{1,0:T(1,128)S(1)} %copy-done.3, f32[]{:T(128)S(6)} %div.27, f32[1,400]{1,0:T(1,128)S(1)} %bitcast.35, f32[1,106496]{1,0:T(1,128)S(1)} %concatenate.30, f32[1,106896]{1,0:T(1,128)S(1)} %copy-done.4, ...), kind=kLoop, calls=%fused_computation.22 | loop fusion | flops 2137920 | bytes 3206884 | tf_op jit(solution)/shard_map/convert.2
  78.7 0.0 copy-start
  78.7 1.2 %slice_reduce_fusion = bf16[106496]{0:T(1024)(128)(2,1)S(1)} fusion(bf16[1,106896]{1,0:T(2,128)(2,1)S(1)} %get-tuple-element.10), kind=kLoop, calls=%fused_computation.17 | loop fusion | bytes 425984 | tf_op jit(solution)/shard_map/slice | solution.py:139
  80.0 0.2 stack.9
  80.2 0.0 copy-start.2
  80.2 0.2 copy.35
  80.3 0.0 copy-done
  80.4 0.8 copy-done.2
  81.2 0.7 multiply_add_fusion
  81.9 0.0 copy-start.1
  81.9 1.1 fusion.2
  83.0 0.2 stack.10
  83.3 0.0 copy-done.1
  83.3 0.2 copy.36
  83.4 0.2 maximum_bitcast_fusion
  83.6 0.6 reshape.126
  84.2 0.1 pad_maximum_fusion.1
  84.4 0.5 broadcast.80
  84.9 0.9 reduce.7
  85.8 0.3 reshape.135
  86.1 20.0 %all_to_all.21 = bf16[32,2,3584]{2,1,0:T(2,128)(2,1)S(1)} all-to-all(bf16[32,2,3584]{2,1,0:T(2,128)(2,1)S(1)} %reshape.135), channel_id=1, replica_groups=mesh['rep'=16,'shard'=32] {'shard'}, dimensions={0} | all-to-all | bytes 917504 | tf_op jit(solution)/shard_map/all_to_all | solution.py:149
  106.1 0.4 reshape.136
  106.5 0.2 copy.43
  106.7 0.7 reshape.129
  107.4 0.8 reshape.127
  108.2 1.8 %copy.38 = bf16[2,32,52,64]{2,1,3,0:T(8,128)(2,1)S(1)} copy(bf16[2,32,52,64]{3,2,0,1:T(8,128)(2,1)S(1)} %bitcast.26) | data formatting | bytes 851968 | tf_op jit(solution)/shard_map/transpose | solution.py:151
  110.0 2.7 %reshape.128 = bf16[2,1664,64]{1,2,0:T(8,128)(2,1)} reshape(bf16[2,32,52,64]{2,1,3,0:T(8,128)(2,1)S(1)} %copy.38) | data formatting | bytes 851968 | tf_op jit(solution)/shard_map/reshape | solution.py:151
  (11 shorter events, 0.3 us)
Async XLA Ops:
  2.7 0.7 copy-start.6
  33.1 36.8 %all-to-all-start = ((f32[512,1,256]{2,1,0:T(1,128)}), f32[512,1,256]{2,1,0:T(1,128)S(1)}, u32[]{:S(2)}, u32[]{:S(2)}) async-start(f32[512,1,256]{2,1,0:T(1,128)} %all_to_all.14), calls=%async_computation | async-start | bytes 1048576 | tf_op jit(solution)/shard_map/all_to_all | solution.py:117
  72.4 1.0 copy-start.5
  72.6 1.0 copy-start.3
  72.6 1.2 %copy-start.4 = (f32[1,106896]{1,0:T(1,128)S(1)}, f32[1,106896]{1,0:T(1,128)}, u32[]{:S(2)}) copy-start(f32[1,106896]{1,0:T(1,128)} %param.9) | copy-start | bytes 1282756
  78.7 1.6 %copy-start = (f32[1,106896]{1,0:T(1,128)}, f32[1,106896]{1,0:T(1,128)S(1)}, u32[]{:S(2)}) copy-start(f32[1,106896]{1,0:T(1,128)S(1)} %get-tuple-element.11) | copy-start | bytes 1282756
  80.2 1.0 copy-start.2
  81.9 1.3 %copy-start.1 = (f32[1,106896]{1,0:T(1,128)}, f32[1,106896]{1,0:T(1,128)S(1)}, u32[]{:S(2)}) copy-start(f32[1,106896]{1,0:T(1,128)S(1)} %multiply_add_fusion) | copy-start | bytes 1282756

commit v8 on v7

--- a/solution.py
+++ b/solution.py
@@ -114,6 +114,9 @@
         ((0, 0), (0, width2 - sub - 1)),
     )
     send2 = jnp.broadcast_to(rowdata[None], (replicas, owners, width2)).reshape(replicas * owners, width2)
+    kept_first, kept_second, kept_ema = lax.optimization_barrier(
+        (beta_one * first_moment, beta_two * second_moment, ema_keep * ema_flat)
+    )
     got2 = lax.all_to_all(send2, ("rep", "shard"), split_axis=0, concat_axis=0, tiled=True)
     got2 = got2.reshape(replicas, owners, width2)
     total = jnp.sum(got2[:, :, sub]) / (replicas * replicas)
@@ -125,8 +128,8 @@
     rms = jnp.sqrt(total / PARAMS)
     clip = jnp.minimum(1.0, 1.0 / (rms + clip_eps))
     clipped = grads * (clip / replicas)
-    new_first = beta_one * first_moment + (1.0 - beta_one) * clipped
-    new_second = beta_two * second_moment + (1.0 - beta_two) * clipped * clipped
+    new_first = kept_first + (1.0 - beta_one) * clipped
+    new_second = kept_second + (1.0 - beta_two) * clipped * clipped
     update = (
         new_first
         / (1.0 - beta_one**STEP)
@@ -135,7 +138,7 @@
     column = jnp.arange(grads.shape[1], dtype=jnp.int32)[None, :]
     decayed = jnp.where(column < main_len, weight_decay * master_flat, 0.0)
     new_master = master_flat - learn_rate * (update + decayed)
-    new_ema = ema_keep * ema_flat + (1.0 - ema_keep) * new_master
+    new_ema = kept_ema + (1.0 - ema_keep) * new_master
     weights = new_master[0, :main_len].astype(jnp.bfloat16)
     averaged = new_ema[0, :main_len].astype(jnp.bfloat16)
     stacked = jnp.stack([weights, averaged], axis=0).reshape(2, own_rows, owners, cols)

time: 115 us -> 114 us (level)
  waiting for transfers between devices: 20.1 us -> 18 us
  other arithmetic: 8.35 us -> 10.1 us
    all_to_all x1, waiting for transfers between devices: 20.1 us -> 18 us  [shards(): lax.all_to_all(send2, ('rep', 'shard'), split_axis=0, concat_axis=0, tile...]
    mul x0 -> x2, other arithmetic: none -> 2.08 us  [the longest x1 1.64 us: shards(): ema_keep * ema_flat]
    unnamed x21 -> x23, local copies, waits for them, and re-layouts: 4.91 us -> 4.07 us
  transfers between devices with their start and end apart: 1 -> 1, of which waited for: 1 -> 1; matrix products, arithmetic and copies ran while one was open for 1% -> 2% of each run, Pallas kernels for 0% -> 0%
where the time goes in v8:
time: 114 us; the launch traced here: 112 us
  Pallas kernels  24.7 us (22%)
  local copies, waits for them, and re-layouts  21.1 us (19%)
  blocking collectives  20 us (18%)
  waiting for transfers between devices  18 us (16%)
  starting transfers between devices  16 us (14%)
  other arithmetic  10.1 us (9%)
  between operations  1.68 us (1%)
    pallas_call x1, Pallas kernels, reduce_scatter(): pl.pallas_call(functools.partial(_rs_kernel, n, main, share), out_shape=(...  24.7 us
    all_to_all x1, blocking collectives, shards(): lax.all_to_all(send2, 'shard', split_axis=0, concat_axis=0, tiled=True)  20 us
    all_to_all x1, waiting for transfers between devices, shards(): lax.all_to_all(send2, ('rep', 'shard'), split_axis=0, concat_axis=0, tile...  18 us
    all_to_all x1, starting transfers between devices, shards(): lax.all_to_all(send2, ('rep', 'shard'), split_axis=0, concat_axis=0, tile...  16 us
    another operation x1, other arithmetic  4.75 us
    unnamed x23, local copies, waits for them, and re-layouts  4.07 us
    reshape x2, local copies, waits for them, and re-layouts, shards(): got2[:, :2 * piece].reshape(owners, 2, own_rows, cols).transpose(1, 0, 2, 3)  3.43 us
  transfers between devices with their start and end apart: 1, of which 1 were waited for; matrix products, arithmetic and copies ran while one was open for 2% of the time, Pallas kernels for 0%

profile of v8, /device:TPU:6, one launch (start us, length us, event | category | flops | bytes accessed | tf_op | source)
XLA Modules:
  0.0 111.5 jit_solution(1324194903125014093)
XLA Ops:
  0.6 1.3 %copy.31 = f32[1,1664,64]{2,1,0:T(8,128)S(1)} copy(f32[1,1664,64]{1,2,0:T(8,128)} %param.6) | data formatting | bytes 851968 | tf_op args[0]
  1.9 0.4 reshape_squeeze.3
  2.3 0.3 copy.32
  2.7 0.0 copy-start.7
  2.7 0.3 reshape.120
  3.0 0.4 copy-done.7
  3.4 0.9 copy.41
  4.3 24.7 %shard_map.109 = (f32[56,128]{1,0:T(8,128)}, f32[8,128]{1,0:T(8,128)}) custom-call(f32[16,56,128]{2,1,0:T(8,128)} %bitcast.30), custom_call_target="tpu_custom_call" | custom-call | tf_op jit(solution)/shard_map/pallas_call | solution.py:74
  29.0 1.2 %slice.35 = f32[1,1]{1,0:T(1,128)} slice(f32[8,128]{1,0:T(8,128)} %get-tuple-element.13), slice={[0:1], [0:1]} | slice | bytes 8 | tf_op jit(solution)/shard_map/slice | solution.py:110
  30.2 0.8 reshape.122
  31.1 0.7 pad_select_fusion
  31.8 1.3 %all_to_all.14 = f32[512,1,256]{2,1,0:T(1,128)} reshape(f32[16,32,256]{2,1,0:T(8,128)S(1)} %broadcast_in_dim.29) | data formatting | bytes 1048576 | tf_op jit(solution)/shard_map/all_to_all | solution.py:120
  33.1 0.0 copy-start.5
  33.1 0.0 copy-start.6
  33.1 16.0 %all-to-all-start = ((f32[512,1,256]{2,1,0:T(1,128)}), f32[512,1,256]{2,1,0:T(1,128)S(1)}, u32[]{:S(2)}, u32[]{:S(2)}) async-start(f32[512,1,256]{2,1,0:T(1,128)} %all_to_all.14), calls=%async_computation | async-start | bytes 1048576 | tf_op jit(solution)/shard_map/all_to_all | solution.py:120
  49.1 0.0 copy-done.5
  49.1 0.0 copy-done.6
  49.1 0.0 copy-start.3
  49.1 1.6 %broadcast_multiply_fusion = (f32[1,106896]{1,0:T(1,128)S(1)}, f32[1,106896]{1,0:T(1,128)}) fusion(f32[1,106896]{1,0:T(1,128)S(1)} %copy-done.5, f32[1,106896]{1,0:T(1,128)S(1)} %copy-done.6), kind=kLoop, calls=%fused_computation.19 | loop fusion | flops 213792 | bytes 1710336 | tf_op jit(solution)/shard_map/mul | solution.py:118
  50.8 0.0 copy-done.3
  50.8 0.4 broadcast_multiply_fusion.2
  51.2 0.7 slice.45
  51.9 18.0 %all-to-all-done = f32[512,1,256]{2,1,0:T(1,128)S(1)} async-done(((f32[512,1,256]{2,1,0:T(1,128)}), f32[512,1,256]{2,1,0:T(1,128)S(1)}, u32[]{:S(2)}, u32[]{:S(2)}) %all-to-all-start) | async-done | bytes 524320 | tf_op jit(solution)/shard_map/all_to_all | solution.py:120
  69.9 0.7 slice_reduce_fusion.1
  71.4 0.3 copy.33
  71.7 0.6 reshape.124
  72.4 0.2 copy.34
  72.6 0.0 copy-start.1
  72.6 0.0 copy-start.4
  72.6 0.5 concatenate.30
  73.1 0.4 copy-done.1
  73.6 0.1 copy-done.4
  73.7 4.8 %fusion.3 = (bf16[1,106896]{1,0:T(2,128)(2,1)S(1)}, f32[1,106896]{1,0:T(1,128)S(1)}, f32[1,106896]{1,0:T(1,128)}, f32[1,106896]{1,0:T(1,128)}) fusion(f32[1,106896]{1,0:T(1,128)S(1)} %copy-done.4, f32[1,106896]{1,0:T(1,128)S(1)} %copy-done.1, f32[]{:T(128)S(6)} %div.27, f32[1,400]{1,0:T(1,128)S(1)} %bitcast.35, f32[1,106496]{1,0:T(1,128)S(1)} %concatenate.30, ...), kind=kLoop, calls=%fused_computation.25 | loop fusion | flops 1924128 | bytes 3206884 | tf_op jit(solution)/shard_map/convert.2
  78.4 0.0 copy-start
  78.5 1.2 %slice_reduce_fusion = bf16[106496]{0:T(1024)(128)(2,1)S(1)} fusion(bf16[1,106896]{1,0:T(2,128)(2,1)S(1)} %get-tuple-element.16), kind=kLoop, calls=%fused_computation.17 | loop fusion | bytes 425984 | tf_op jit(solution)/shard_map/slice | solution.py:142
  79.7 0.2 stack.9
  79.9 0.2 copy.35
  80.1 0.0 copy-done
  80.1 0.6 multiply_add_fusion
  80.7 0.0 copy-start.2
  80.7 1.1 %fusion.2 = bf16[106496]{0:T(1024)(128)(2,1)S(1)} fusion(f32[1,106896]{1,0:T(1,128)S(1)} %multiply_add_fusion), kind=kLoop, calls=%fused_computation.16 | loop fusion | bytes 425984 | tf_op jit(solution)/shard_map/slice | solution.py:143
  81.8 0.2 stack.10
  82.0 0.0 copy-done.2
  82.0 0.2 copy.36
  82.2 0.2 maximum_bitcast_fusion
  82.4 0.6 reshape.126
  83.0 0.1 pad_maximum_fusion.1
  83.2 0.5 broadcast.79
  83.7 0.9 reduce.7
  84.6 0.3 reshape.135
  84.9 20.0 %all_to_all.21 = bf16[32,2,3584]{2,1,0:T(2,128)(2,1)S(1)} all-to-all(bf16[32,2,3584]{2,1,0:T(2,128)(2,1)S(1)} %reshape.135), channel_id=1, replica_groups=mesh['rep'=16,'shard'=32] {'shard'}, dimensions={0} | all-to-all | bytes 917504 | tf_op jit(solution)/shard_map/all_to_all | solution.py:152
  104.9 0.4 reshape.136
  105.3 0.2 copy.43
  105.5 0.7 reshape.129
  106.2 0.8 reshape.127
  107.0 1.8 %copy.38 = bf16[2,32,52,64]{2,1,3,0:T(8,128)(2,1)S(1)} copy(bf16[2,32,52,64]{3,2,0,1:T(8,128)(2,1)S(1)} %bitcast.26) | data formatting | bytes 851968 | tf_op jit(solution)/shard_map/transpose | solution.py:154
  108.8 2.7 %reshape.128 = bf16[2,1664,64]{1,2,0:T(8,128)(2,1)} reshape(bf16[2,32,52,64]{2,1,3,0:T(8,128)(2,1)S(1)} %copy.38) | data formatting | bytes 851968 | tf_op jit(solution)/shard_map/reshape | solution.py:154
  (11 shorter events, 0.3 us)
Async XLA Ops:
  2.7 0.7 copy-start.7
  33.1 16.0 %copy-start.5 = (f32[1,106896]{1,0:T(1,128)S(1)}, f32[1,106896]{1,0:T(1,128)}, u32[]{:S(2)}) copy-start(f32[1,106896]{1,0:T(1,128)} %param.11) | copy-start | bytes 1282756
  33.1 16.0 %copy-start.6 = (f32[1,106896]{1,0:T(1,128)S(1)}, f32[1,106896]{1,0:T(1,128)}, u32[]{:S(2)}) copy-start(f32[1,106896]{1,0:T(1,128)} %param.9) | copy-start | bytes 1282756
  33.1 36.8 %all-to-all-start = ((f32[512,1,256]{2,1,0:T(1,128)}), f32[512,1,256]{2,1,0:T(1,128)S(1)}, u32[]{:S(2)}, u32[]{:S(2)}) async-start(f32[512,1,256]{2,1,0:T(1,128)} %all_to_all.14), calls=%async_computation | async-start | bytes 1048576 | tf_op jit(solution)/shard_map/all_to_all | solution.py:120
  49.1 1.7 %copy-start.3 = (f32[1,106896]{1,0:T(1,128)S(1)}, f32[1,106896]{1,0:T(1,128)}, u32[]{:S(2)}) copy-start(f32[1,106896]{1,0:T(1,128)} %param.8) | copy-start | bytes 1282756
  72.6 1.0 copy-start.1
  72.6 1.1 %copy-start.4 = (f32[1,106896]{1,0:T(1,128)S(1)}, f32[1,106896]{1,0:T(1,128)}, u32[]{:S(2)}) copy-start(f32[1,106896]{1,0:T(1,128)} %param.10) | copy-start | bytes 1282756
  78.4 1.6 %copy-start = (f32[1,106896]{1,0:T(1,128)}, f32[1,106896]{1,0:T(1,128)S(1)}, u32[]{:S(2)}) copy-start(f32[1,106896]{1,0:T(1,128)S(1)} %get-tuple-element.17) | copy-start | bytes 1282756
  80.7 1.3 %copy-start.2 = (f32[1,106896]{1,0:T(1,128)}, f32[1,106896]{1,0:T(1,128)S(1)}, u32[]{:S(2)}) copy-start(f32[1,106896]{1,0:T(1,128)S(1)} %multiply_add_fusion) | copy-start | bytes 1282756
